TPU v7x, 256 devices: a whole 4x4x8 slice. The times are simulated.
256 devices in a mesh: section: 32 (over z_lo, x, core), tensor: 8 (over y, z_hi).
Axes of the slice: x: 4, y: 4, z: 8 (z_hi: 2, z_lo: 4; z = z_hi * 4 + z_lo), core: 2. Of those that a mesh axis runs over, the one named last changes fastest.
Arguments:
- forward_input: bfloat16 [32, 256, 8192], P('section', None, 'tensor'), may hold values from -6 to 6
- saved_last: bfloat16 [32, 256, 8192], P('section', None, 'tensor'), may hold values from -6 to 6
- saved_first: bfloat16 [32, 256, 8192], P('section', None, 'tensor'), may hold values from -6 to 6
- first_cotangent: bfloat16 [32, 256, 8192], P('section', None, 'tensor'), may hold values from -6 to 6
- section_entry: bfloat16 [256, 8192], P(None, 'tensor'), may hold values from -6 to 6
- last_gain: float32 [32, 8192], P('section'), may hold values from 0.1 to 1.9
- last_up: bfloat16 [32, 8192, 1024], P('section', None, 'tensor'), may hold values from -0.0625 to 0.0625
- last_down: bfloat16 [32, 1024, 8192], P('section', 'tensor'), may hold values from -0.1875 to 0.1875
- first_gain: float32 [32, 8192], P('section'), may hold values from 0.1 to 1.9
- first_up: bfloat16 [32, 8192, 1024], P('section', None, 'tensor'), may hold values from -0.0625 to 0.0625
- first_down: bfloat16 [32, 1024, 8192], P('section', 'tensor'), may hold values from -0.1875 to 0.1875
- head_gain: float32 [8192], replicated, may hold values from 0.1 to 1.9
- head_weight: float32 [8192, 4], P('tensor'), may hold values from -0.0625 to 0.0625
- head_bias: float32 [4], replicated, may hold values from -3 to 3
- prompt_length: int32 [1], replicated, may hold values from 8 to 248
- keep_mask: int32 [1, 256], replicated, may hold values 0 or 1
- target_box: int32 [1, 4], replicated, may hold values from 0 to 1000, as said below
Outputs:
- layer_output: bfloat16 [32, 256, 8192], P('section', None, 'tensor')
- input_gradient: bfloat16 [32, 256, 8192], P('section', None, 'tensor')
Inputs may be any that keep to these rules, and one draw needn't show every extreme that they name: `target_box`: each row is a box x1, y1, x2, y2 with x2 - x1 and y2 - y1 at least 100.
All inputs are finite; a program needn't handle non-finite values.
Results may differ from a plain program's by a relative error of at most 0.018.
Values may be sent and summed in bfloat16 or wider, within the bound.
A program may use at most 128 MiB of HBM per device.

v0:
```python
import jax
import jax.numpy as jnp
from jax import lax
from jax.sharding import PartitionSpec as P

epsilon = 1e-06
softness = 4.0
loss_scale = 4096.0


def shifted(value, axis, steps):
    count = lax.axis_size(axis)
    initial, last = (max(0, -steps), min(count, count - steps))
    return lax.ppermute(value, axis, [(source, source + steps) for source in range(initial, last)])


def unit_rows(values):
    values = values.astype(jnp.float32)
    inverse = lax.rsqrt(jnp.mean(values * values, axis=-1, keepdims=True) + epsilon)
    return (values * inverse, inverse)


def column_start(local_width):
    return lax.axis_index("tensor") * local_width


def column_slice(full_rows, local_width):
    return lax.dynamic_slice_in_dim(full_rows, column_start(local_width), local_width, 1)


def gather_columns(local_rows):
    return lax.all_gather(local_rows, "tensor", axis=1, tiled=True)


def reduce_columns(partial_rows):
    return lax.psum_scatter(
        partial_rows.astype(jnp.bfloat16), "tensor", scatter_dimension=1, tiled=True
    ).astype(jnp.float32)


def row_sums(values):
    return lax.psum(values, "tensor")


def layer_core(full_rows, gain_row, up_matrix, down_matrix):
    scaled, inverse = unit_rows(full_rows)
    normed = (scaled * gain_row).astype(jnp.bfloat16)
    activated = jax.nn.silu(jnp.dot(normed, up_matrix, preferred_element_type=jnp.float32)).astype(
        jnp.bfloat16
    )
    return jnp.dot(activated, down_matrix, preferred_element_type=jnp.float32)


def layer_backward(saved_rows, cotangent, gain_row, up_matrix, down_matrix):
    saved_full, cotangent_full = (
        lax.all_gather(saved_rows, "tensor", axis=1, tiled=True),
        lax.all_gather(cotangent, "tensor", axis=1, tiled=True),
    )
    scaled, inverse = unit_rows(saved_full)
    normed = (scaled * gain_row).astype(jnp.bfloat16)
    pre_act = jnp.dot(normed, up_matrix, preferred_element_type=jnp.float32)
    act_grad = lax.dot_general(
        cotangent_full, down_matrix, (((1,), (1,)), ((), ())), preferred_element_type=jnp.float32
    )
    sigmoid_pre = jax.nn.sigmoid(pre_act)
    pre_grad = (act_grad * sigmoid_pre * (1.0 + pre_act * (1.0 - sigmoid_pre))).astype(jnp.bfloat16)
    norm_partial = lax.dot_general(
        pre_grad, up_matrix, (((1,), (1,)), ((), ())), preferred_element_type=jnp.float32
    )
    norm_grad = reduce_columns(norm_partial)
    local_width = cotangent.shape[1]
    full_width = saved_full.shape[1]
    scaled_cols = column_slice(scaled, local_width)
    gain_cols = lax.dynamic_slice_in_dim(gain_row, column_start(local_width), local_width, 0)
    row_total = row_sums(jnp.sum(scaled_cols * gain_cols * norm_grad, axis=1))
    result = cotangent.astype(jnp.float32) + inverse * (
        gain_cols * norm_grad - scaled_cols * row_total[:, None] / full_width
    )
    return result.astype(jnp.bfloat16)


def soft_min(first, second):
    return 0.5 * (
        first + second - jnp.sqrt((first - second) * (first - second) + softness * softness)
    )


def soft_max(first, second):
    return 0.5 * (
        first + second + jnp.sqrt((first - second) * (first - second) + softness * softness)
    )


def soft_relu(difference):
    return 0.5 * (difference + jnp.sqrt(difference * difference + softness * softness))


def box_loss(logits, target_box):
    scaled_box = jax.nn.sigmoid(logits) * 1000.0
    centre_x = scaled_box[:, 0]
    centre_y = scaled_box[:, 1]
    box_width = scaled_box[:, 2]
    box_height = scaled_box[:, 3]
    left_pred = centre_x - 0.5 * box_width
    right_pred = centre_x + 0.5 * box_width
    lower_pred = centre_y - 0.5 * box_height
    upper_pred = centre_y + 0.5 * box_height
    target = target_box.astype(jnp.float32)
    inner_width = soft_relu(soft_min(right_pred, target[:, 2]) - soft_max(left_pred, target[:, 0]))
    inner_height = soft_relu(
        soft_min(upper_pred, target[:, 3]) - soft_max(lower_pred, target[:, 1])
    )
    intersection_area = inner_width * inner_height
    target_area = (target[:, 2] - target[:, 0]) * (target[:, 3] - target[:, 1])
    union_area = box_width * box_height + target_area - intersection_area
    outer_width = soft_max(right_pred, target[:, 2]) - soft_min(left_pred, target[:, 0])
    outer_height = soft_max(upper_pred, target[:, 3]) - soft_min(lower_pred, target[:, 1])
    enclosing = outer_width * outer_height
    return loss_scale * jnp.mean(
        1.0 - intersection_area / union_area + (enclosing - union_area) / enclosing
    )


def head_cotangent(
    final_rows, head_gain, head_weight, head_bias, prompt_length, keep_mask, target_box
):
    row_count = keep_mask.shape[0]
    positions = jnp.arange(keep_mask.shape[1], dtype=jnp.int32)[None, :]
    starts = prompt_length[:, None]
    weights = (positions == starts - 1).astype(jnp.float32) + (positions >= starts).astype(
        jnp.float32
    ) * keep_mask.astype(jnp.float32)
    counts = jnp.sum(weights, axis=1)
    local_width = final_rows.shape[1]
    full_width = local_width * lax.axis_size("tensor")
    tokens = final_rows.astype(jnp.float32).reshape(row_count, keep_mask.shape[1], local_width)
    pooled = (
        jnp.einsum("rt,rtd->rd", weights, tokens, precision=lax.Precision.HIGHEST) / counts[:, None]
    )
    gain_cols = lax.dynamic_slice_in_dim(head_gain, column_start(local_width), local_width, 0)
    logit_part = jnp.dot(pooled * gain_cols, head_weight, precision=lax.Precision.HIGHEST)
    square_part = jnp.sum(pooled * pooled, axis=1, keepdims=True)
    totals = row_sums(jnp.concatenate([logit_part, square_part], axis=1))
    inverse = lax.rsqrt(totals[:, 4] / full_width + epsilon)
    logits = totals[:, :4] * inverse[:, None] + head_bias

    def loss_of(logit_value):
        return box_loss(logit_value, target_box)

    loss_value, pullback = jax.vjp(loss_of, logits)
    logit_grad = pullback(jnp.ones((), jnp.float32))[0]
    scaled_grad = jnp.dot(logit_grad, head_weight.T, precision=lax.Precision.HIGHEST)
    unit_pooled = pooled * inverse[:, None]
    row_total = row_sums(jnp.sum(unit_pooled * gain_cols * scaled_grad, axis=1))
    pooled_grad = inverse[:, None] * (
        gain_cols * scaled_grad - unit_pooled * row_total[:, None] / full_width
    )
    token_grad = (weights / counts[:, None])[:, :, None] * pooled_grad[:, None, :]
    return token_grad.reshape(final_rows.shape[0], local_width).astype(jnp.bfloat16)


def per_device(
    forward_input,
    saved_last,
    saved_first,
    first_cotangent,
    section_entry,
    last_gain,
    last_up,
    last_down,
    first_gain,
    first_up,
    first_down,
    head_gain,
    head_weight,
    head_bias,
    prompt_length,
    keep_mask,
    target_box,
):
    section_index = lax.axis_index("section")
    opening = section_index == 0
    closing = section_index == lax.axis_size("section") - 1
    local_input = forward_input[0]
    gathered_input = gather_columns(local_input)
    last_partial = layer_core(gathered_input, last_gain[0], last_up[0], last_down[0])
    hidden_local = (local_input.astype(jnp.float32) + reduce_columns(last_partial)).astype(
        jnp.bfloat16
    )
    arrived_local = shifted(hidden_local, "section", 1)
    entry_local = jnp.where(opening, section_entry, arrived_local)
    entry_full = gather_columns(entry_local)
    first_partial = layer_core(entry_full, first_gain[0], first_up[0], first_down[0])
    layer_output = (entry_local.astype(jnp.float32) + reduce_columns(first_partial)).astype(
        jnp.bfloat16
    )
    first_grad = layer_backward(
        saved_first[0], first_cotangent[0], first_gain[0], first_up[0], first_down[0]
    )
    returned = shifted(first_grad, "section", -1)
    head_grad = head_cotangent(
        hidden_local, head_gain, head_weight, head_bias, prompt_length, keep_mask, target_box
    )
    cotangent = jnp.where(closing, head_grad, returned)
    saved_rows = jnp.where(closing, local_input, saved_last[0])
    input_gradient = layer_backward(saved_rows, cotangent, last_gain[0], last_up[0], last_down[0])
    return (layer_output[None], input_gradient[None])


def solution(mesh):
    placed = (
        P("section", None, "tensor"),
        P("section", None, "tensor"),
        P("section", None, "tensor"),
        P("section", None, "tensor"),
        P(None, "tensor"),
        P("section", None),
        P("section", None, "tensor"),
        P("section", "tensor", None),
        P("section", None),
        P("section", None, "tensor"),
        P("section", "tensor", None),
        P(),
        P("tensor", None),
        P(),
        P(),
        P(),
        P(),
    )
    return jax.shard_map(
        per_device,
        mesh=mesh,
        in_specs=placed,
        out_specs=(P("section", None, "tensor"), P("section", None, "tensor")),
        check_vma=False,
    )
```

profile of v0, /device:TPU:38, one launch (start us, length us, event | category | flops | bytes accessed | tf_op | source)
XLA Modules:
  0.0 1163.7 jit_solution(11418929649073457624)
XLA Ops:
  7.2 0.7 all-gather.15.cloned.1.call-update
  8.0 0.7 all-gather.17.cloned.1.call-update
  8.7 0.7 all-gather.19.cloned.1.call-update
  9.5 109.8 %all-gather.15.cloned.1.call-done = bf16[1,256,8192]{2,1,0:T(8,128)(2,1)} async-done(((bf16[1,256,1024]{2,1,0:T(8,128)(2,1)}), bf16[1,256,8192]{2,1,0:T(8,128)(2,1)}) %all-gather.15.cloned.1.call-update) | async-done | bytes 4194320 | tf_op jit(solution)/shard_map/all_gather | solution.py:32
  119.3 3.1 fusion.3
  122.4 7.4 convolution_convert_fusion.3
  129.9 93.7 %all-gather.17.cloned.1.call-done = bf16[1,256,8192]{2,1,0:T(8,128)(2,1)} async-done(((bf16[1,256,1024]{2,1,0:T(8,128)(2,1)}), bf16[1,256,8192]{2,1,0:T(8,128)(2,1)}) %all-gather.17.cloned.1.call-update) | async-done | bytes 4194320 | tf_op jit(solution)/shard_map/all_gather | solution.py:56
  223.6 3.3 fusion.6
  227.0 3.0 fusion.8
  230.1 97.9 %all-gather.19.cloned.1.call-done = bf16[1,256,8192]{2,1,0:T(8,128)(2,1)} async-done(((bf16[1,256,1024]{2,1,0:T(8,128)(2,1)}), bf16[1,256,8192]{2,1,0:T(8,128)(2,1)}) %all-gather.19.cloned.1.call-update) | async-done | bytes 4194320 | tf_op jit(solution)/shard_map/all_gather | solution.py:57
  327.9 9.9 convolution_convert_fusion.1
  338.0 0.9 copy-done.3
  339.1 0.8 broadcast_select_fusion
  344.5 108.8 %reduce-scatter.5.cloned.1.call-done = bf16[256,1024]{1,0:T(8,128)(2,1)} async-done(((bf16[256,8192]{1,0:T(8,128)(2,1)}), bf16[256,1024]{1,0:T(8,128)(2,1)}) %reduce-scatter.5.cloned.1.call-update) | async-done | bytes 524304 | tf_op jit(solution)/shard_map/reduce_scatter | solution.py:36
  453.3 1.2 fusion.74
  454.9 1.9 dynamic-slice_multiply_fusion
  456.9 0.8 pad_maximum_fusion
  457.7 6.6 convert_multiply_fusion.2
  464.2 31.0 %psum.28 = f32[1,5]{1,0:T(1,128)S(1)} all-reduce(f32[1,5]{1,0:T(1,128)S(1)} %pad_maximum_fusion), channel_id=1, replica_groups=mesh['section'=32,'tensor'=8] {'tensor'}, use_global_device_ids=true, to_apply=%region_6.7 | all-reduce | flops 5 | bytes 40 | tf_op jit(solution)/shard_map/psum | solution.py:42
  496.6 0.7 fusion.140
  509.7 2.0 multiply_reduce_fusion
  511.7 69.3 %reduce-scatter.9.cloned.1.call-done = bf16[256,1024]{1,0:T(8,128)(2,1)} async-done(((bf16[256,8192]{1,0:T(8,128)(2,1)}), bf16[256,1024]{1,0:T(8,128)(2,1)}) %reduce-scatter.9.cloned.1.call-update) | async-done | bytes 524304 | tf_op jit(solution)/shard_map/reduce_scatter | solution.py:36
  580.9 1.6 fusion.68
  582.5 29.9 %all-reduce.4 = (f32[256]{0:T(256)S(1)}, f32[]{:T(128)}) all-reduce(f32[256]{0:T(256)S(1)} %fusion.68, f32[]{:T(128)} %multiply_reduce_fusion), channel_id=1, replica_groups=mesh['section'=32,'tensor'=8] {'tensor'}, use_global_device_ids=true, to_apply=%region_12.13 | all-reduce | flops 257 | bytes 2056 | tf_op jit(solution)/shard_map/psum | solution.py:42
  612.4 1.7 fusion.67
  614.2 1.9 collective-permute-start.1
  616.7 1.9 subtract_multiply_fusion
  618.7 4.1 collective-permute-done.1
  622.8 0.8 copy-done.6
  623.6 1.0 fusion.76
  624.7 3.7 collective-permute-start
  628.4 7.0 collective-permute-done
  635.3 0.9 broadcast_select_fusion.1
  636.3 50.7 %all-gather.21.cloned.1.call-done = bf16[1,256,8192]{2,1,0:T(8,128)(2,1)} async-done(((bf16[1,256,1024]{2,1,0:T(8,128)(2,1)}), bf16[1,256,8192]{2,1,0:T(8,128)(2,1)}) %all-gather.21.cloned.1.call-update) | async-done | bytes 4194320 | tf_op jit(solution)/shard_map/all_gather | solution.py:56
  686.9 3.3 fusion.7
  690.4 1.4 fusion.9
  691.8 104.2 %all-gather.13.cloned.1.call-done = bf16[256,8192]{1,0:T(8,128)(2,1)} async-done(((bf16[256,1024]{1,0:T(8,128)(2,1)}), bf16[256,8192]{1,0:T(8,128)(2,1)}) %all-gather.13.cloned.1.call-update) | async-done | bytes 4194320 | tf_op jit(solution)/shard_map/all_gather | solution.py:57
  796.0 9.3 convolution_convert_fusion
  805.7 95.3 %all-gather.11.cloned.1.call-done = bf16[256,8192]{1,0:T(8,128)(2,1)} async-done(((bf16[256,1024]{1,0:T(8,128)(2,1)}), bf16[256,8192]{1,0:T(8,128)(2,1)}) %all-gather.11.cloned.1.call-update) | async-done | bytes 4194320 | tf_op jit(solution)/shard_map/all_gather | solution.py:32
  900.9 3.1 fusion
  904.1 8.0 convolution_convert_fusion.2
  912.1 6.8 convert_multiply_fusion
  918.9 108.1 %reduce-scatter.11.cloned.1.call-done = bf16[256,1024]{1,0:T(8,128)(2,1)} async-done(((bf16[256,8192]{1,0:T(8,128)(2,1)}), bf16[256,1024]{1,0:T(8,128)(2,1)}) %reduce-scatter.11.cloned.1.call-update) | async-done | bytes 524304 | tf_op jit(solution)/shard_map/reduce_scatter | solution.py:36
  1027.0 1.6 fusion.73
  1028.6 28.3 %psum.31 = f32[256]{0:T(256)S(1)} all-reduce(f32[256]{0:T(256)S(1)} %fusion.73), channel_id=1, replica_groups=mesh['section'=32,'tensor'=8] {'tensor'}, use_global_device_ids=true, to_apply=%region_16.17 | all-reduce | flops 256 | bytes 2048 | tf_op jit(solution)/shard_map/psum | solution.py:42
  1057.0 2.6 fusion.77
  1059.6 95.2 %reduce-scatter.7.cloned.1.call-done = bf16[256,1024]{1,0:T(8,128)(2,1)} async-done(((bf16[256,8192]{1,0:T(8,128)(2,1)}), bf16[256,1024]{1,0:T(8,128)(2,1)}) %reduce-scatter.7.cloned.1.call-update) | async-done | bytes 524304 | tf_op jit(solution)/shard_map/reduce_scatter | solution.py:36
  1154.8 2.0 fusion.75
  (60 shorter events, 4.6 us)
Async XLA Ops:
  7.2 115.2 %copy-start = (bf16[1,8192,128]{2,1,0:T(8,128)(2,1)S(1)}, bf16[1,8192,128]{2,1,0:T(8,128)(2,1)}, u32[]{:S(2)}) copy-start(bf16[1,8192,128]{2,1,0:T(8,128)(2,1)} %param.23) | copy-start | bytes 6291460
  7.2 115.2 %copy-start.10 = (f32[1,8192]{1,0:T(1,128)S(1)}, f32[1,8192]{1,0:T(1,128)}, u32[]{:S(2)}) copy-start(f32[1,8192]{1,0:T(1,128)} %param.22) | copy-start | bytes 98308
  7.2 112.1 %all-gather.15.cloned.1.call-start = ((), (), s32[]{:S(2)}) async-start(), calls=%async_computation.10 | async-start | bytes 4718592 | tf_op jit(solution)/shard_map/all_gather | solution.py:32
  7.9 215.7 %all-gather.17.cloned.1.call-start = ((), (), s32[]{:S(2)}) async-start(), calls=%async_computation.11 | async-start | bytes 4718592 | tf_op jit(solution)/shard_map/all_gather | solution.py:56
  8.7 319.3 %all-gather.19.cloned.1.call-start = ((), (), s32[]{:S(2)}) async-start(), calls=%async_computation.12 | async-start | bytes 4718592 | tf_op jit(solution)/shard_map/all_gather | solution.py:57
  9.4 443.9 %reduce-scatter.5.cloned.1.call-start = ((), (), s32[]{:S(2)}) async-start(), calls=%async_computation.4 | async-start | bytes 4718592 | tf_op jit(solution)/shard_map/reduce_scatter | solution.py:36
  129.8 97.1 %copy-start.9 = (f32[1,8192]{1,0:T(1,128)S(1)}, f32[1,8192]{1,0:T(1,128)}, u32[]{:S(2)}) copy-start(f32[1,8192]{1,0:T(1,128)} %param.25) | copy-start | bytes 98308
  129.8 451.1 %reduce-scatter.9.cloned.1.call-start = ((), (), s32[]{:S(2)}) async-start(), calls=%async_computation.7 | async-start | bytes 4718592 | tf_op jit(solution)/shard_map/reduce_scatter | solution.py:36
  223.6 3.4 copy-start.2
  337.9 1.0 copy-start.3
  337.9 1.2 copy-start.8
  337.9 2.8 copy-start.14
  337.9 6.0 copy-start.12
  337.9 118.9 %copy-start.11 = (f32[1024,4]{0,1:T(4,128)S(1)}, f32[1024,4]{0,1:T(4,128)}, u32[]{:S(2)}) copy-start(f32[1024,4]{0,1:T(4,128)} %param.29) | copy-start | bytes 49156
  337.9 349.0 %all-gather.21.cloned.1.call-start = ((), (), s32[]{:S(2)}) async-start(), calls=%async_computation.13 | async-start | bytes 4718592 | tf_op jit(solution)/shard_map/all_gather | solution.py:56
  339.9 456.1 %all-gather.13.cloned.1.call-start = ((), (), s32[]{:S(2)}) async-start(), calls=%async_computation.8 | async-start | bytes 4718592 | tf_op jit(solution)/shard_map/all_gather | solution.py:57
  457.7 38.9 %copy-start.13 = (f32[4]{0:T(128)S(1)}, f32[4]{0:T(128)}, u32[]{:S(2)}) copy-start(f32[4]{0:T(128)} %param.30) | copy-start | bytes 52
  457.7 154.7 %copy-start.5 = (bf16[1,256,1024]{2,1,0:T(8,128)(2,1)S(1)}, bf16[1,256,1024]{2,1,0:T(8,128)(2,1)}, u32[]{:S(2)}) copy-start(bf16[1,256,1024]{2,1,0:T(8,128)(2,1)} %param.20) | copy-start | bytes 1572868
  614.2 8.6 collective-permute-start.1
  622.8 0.8 copy-start.6
  624.6 276.3 %all-gather.11.cloned.1.call-start = ((), (), s32[]{:S(2)}) async-start(), calls=%async_computation.5 | async-start | bytes 4718592 | tf_op jit(solution)/shard_map/all_gather | solution.py:32
  624.7 10.7 collective-permute-start
  636.2 390.8 %reduce-scatter.11.cloned.1.call-start = ((), (), s32[]{:S(2)}) async-start(), calls=%async_computation.9 | async-start | bytes 4718592 | tf_op jit(solution)/shard_map/reduce_scatter | solution.py:36
  686.9 3.4 copy-start.1
  805.4 349.4 %reduce-scatter.7.cloned.1.call-start = ((), (), s32[]{:S(2)}) async-start(), calls=%async_computation.6 | async-start | bytes 4718592 | tf_op jit(solution)/shard_map/reduce_scatter | solution.py:36
  912.1 144.9 %copy-start.7 = (bf16[256,1024]{1,0:T(8,128)(2,1)S(1)}, bf16[256,1024]{1,0:T(8,128)(2,1)}, u32[]{:S(2)}) copy-start(bf16[256,1024]{1,0:T(8,128)(2,1)} %copy-done.6) | copy-start | bytes 1572868
  918.9 235.9 %copy-start.4 = (bf16[256,1024]{1,0:T(8,128)(2,1)S(1)}, bf16[256,1024]{1,0:T(8,128)(2,1)}, u32[]{:S(2)}) copy-start(bf16[256,1024]{1,0:T(8,128)(2,1)} %broadcast_select_fusion.1) | copy-start | bytes 1572868
Sparse Core Ops, SparseCore 0:
  10.7 108.5 all-gather.14
  121.9 101.6 all-gather.16
  226.2 101.6 all-gather.18
  332.0 121.2 reduce-scatter.4
  457.3 123.5 reduce-scatter.8
  584.0 102.9 all-gather.20
  689.6 106.4 all-gather.12
  799.3 101.6 all-gather.10
  905.1 121.8 reduce-scatter.10
  1031.1 123.7 reduce-scatter.6
where the time goes:
time: 1170 us; the launch traced here: 1160 us
  waiting for transfers between devices  946 us (81%)
  blocking collectives  89.3 us (8%)
  other arithmetic  47.5 us (4%)
  matrix products  39.8 us (3%)
  between operations  30.4 us (3%)
    reduce_scatter x4, waiting for transfers between devices, reduce_columns(): lax.psum_scatter(partial_rows.astype(jnp.bfloat16), 'tensor', scatter_dim...  381 us
    all_gather x2, waiting for transfers between devices, gather_columns(): return lax.all_gather(local_rows, 'tensor', axis=1, tiled=True)  205 us
    all_gather x2, waiting for transfers between devices, layer_backward(): lax.all_gather(cotangent, 'tensor', axis=1, tiled=True)  202 us
    all_gather x2, waiting for transfers between devices, layer_backward(): lax.all_gather(saved_rows, 'tensor', axis=1, tiled=True)  144 us
    psum x3, blocking collectives, row_sums(): return lax.psum(values, 'tensor')  89.3 us
  transfers between devices with their start and end apart: 12, of which 12 were waited for; matrix products, arithmetic and copies ran while one was open for 7% of the time, Pallas kernels for 0%

commit v1 on v0

--- a/solution.py
+++ b/solution.py
@@ -1,11 +1,17 @@
+import functools
+
 import jax
 import jax.numpy as jnp
 from jax import lax
+from jax.experimental import pallas as pl
+from jax.experimental.pallas import tpu as pltpu
+from jax.sharding import Mesh
 from jax.sharding import PartitionSpec as P
 
 epsilon = 1e-06
 softness = 4.0
 loss_scale = 4096.0
+TENSOR = ("ty", "tz")
 
 
 def shifted(value, axis, steps):
@@ -14,6 +20,14 @@
     return lax.ppermute(value, axis, [(source, source + steps) for source in range(initial, last)])
 
 
+def tensor_size():
+    return lax.axis_size("ty") * lax.axis_size("tz")
+
+
+def tensor_index():
+    return lax.axis_index("ty") * lax.axis_size("tz") + lax.axis_index("tz")
+
+
 def unit_rows(values):
     values = values.astype(jnp.float32)
     inverse = lax.rsqrt(jnp.mean(values * values, axis=-1, keepdims=True) + epsilon)
@@ -21,25 +35,231 @@
 
 
 def column_start(local_width):
-    return lax.axis_index("tensor") * local_width
+    return tensor_index() * local_width
 
 
 def column_slice(full_rows, local_width):
     return lax.dynamic_slice_in_dim(full_rows, column_start(local_width), local_width, 1)
 
 
-def gather_columns(local_rows):
-    return lax.all_gather(local_rows, "tensor", axis=1, tiled=True)
-
-
-def reduce_columns(partial_rows):
-    return lax.psum_scatter(
-        partial_rows.astype(jnp.bfloat16), "tensor", scatter_dimension=1, tiled=True
-    ).astype(jnp.float32)
+MESH_ID = pl.DeviceIdType.MESH
+
+
+def gather_kernel(ny, nz, x_ref, out_ref, send_sems, recv_sems):
+    width = x_ref.shape[2]
+    ty, tz = lax.axis_index("ty"), lax.axis_index("tz")
+    me = ty * nz + tz
+    partner_z = 1 - tz
+    partner = ty * nz + partner_z
+    y_peers = [lax.rem(ty + step, ny) for step in range(1, ny)]
+    section = lax.axis_index("section")
+
+    def device(y, z):
+        return (section, y, z)
+
+    def cols(index):
+        return pl.ds(pl.multiple_of(index * width, width), width)
+
+    barrier = pltpu.get_barrier_semaphore()
+    pl.semaphore_signal(barrier, inc=1, device_id=device(ty, partner_z), device_id_type=MESH_ID)
+    for y in y_peers:
+        pl.semaphore_signal(barrier, inc=1, device_id=device(y, tz), device_id_type=MESH_ID)
+    pl.semaphore_wait(barrier, ny)
+
+    sends = [
+        pltpu.make_async_remote_copy(
+            src_ref=x_ref,
+            dst_ref=out_ref.at[:, :, cols(me)],
+            send_sem=send_sems.at[0],
+            recv_sem=recv_sems.at[me],
+            device_id=device(ty, partner_z),
+            device_id_type=MESH_ID,
+        )
+    ]
+    for number, y in enumerate(y_peers):
+        sends.append(
+            pltpu.make_async_remote_copy(
+                src_ref=x_ref,
+                dst_ref=out_ref.at[:, :, cols(me)],
+                send_sem=send_sems.at[1 + number],
+                recv_sem=recv_sems.at[me],
+                device_id=device(y, tz),
+                device_id_type=MESH_ID,
+            )
+        )
+    for copy in sends:
+        copy.start()
+    out_ref[:, :, cols(me)] = x_ref[...]
+    pltpu.make_async_remote_copy(
+        src_ref=x_ref,
+        dst_ref=out_ref.at[:, :, cols(partner)],
+        send_sem=send_sems.at[0],
+        recv_sem=recv_sems.at[partner],
+        device_id=device(ty, partner_z),
+        device_id_type=MESH_ID,
+    ).wait_recv()
+    forwards = []
+    for number, y in enumerate(y_peers):
+        forwards.append(
+            pltpu.make_async_remote_copy(
+                src_ref=out_ref.at[:, :, cols(partner)],
+                dst_ref=out_ref.at[:, :, cols(partner)],
+                send_sem=send_sems.at[ny + number],
+                recv_sem=recv_sems.at[partner],
+                device_id=device(y, tz),
+                device_id_type=MESH_ID,
+            )
+        )
+    for copy in forwards:
+        copy.start()
+    for y in y_peers:
+        for z in range(nz):
+            source = y * nz + z
+            pltpu.make_async_remote_copy(
+                src_ref=x_ref,
+                dst_ref=out_ref.at[:, :, cols(source)],
+                send_sem=send_sems.at[0],
+                recv_sem=recv_sems.at[source],
+                device_id=device(y, z),
+                device_id_type=MESH_ID,
+            ).wait_recv()
+    for copy in sends + forwards:
+        copy.wait_send()
+
+
+def gather_columns(local_rows, collective):
+    k, rows, width = local_rows.shape
+    ny, nz = lax.axis_size("ty"), lax.axis_size("tz")
+    full = width * ny * nz
+    moved = local_rows.size * local_rows.dtype.itemsize * 7
+    return pl.pallas_call(
+        functools.partial(gather_kernel, ny, nz),
+        out_shape=jax.ShapeDtypeStruct((k, rows, full), local_rows.dtype),
+        in_specs=[pl.BlockSpec(memory_space=pltpu.VMEM)],
+        out_specs=pl.BlockSpec(memory_space=pltpu.VMEM),
+        scratch_shapes=[
+            pltpu.SemaphoreType.DMA((2 * ny - 1,)),
+            pltpu.SemaphoreType.DMA((ny * nz,)),
+        ],
+        compiler_params=pltpu.CompilerParams(
+            collective_id=collective, has_side_effects=True, vmem_limit_bytes=48 * 1024 * 1024
+        ),
+        cost_estimate=pl.CostEstimate(flops=0, transcendentals=0, bytes_accessed=moved),
+    )(local_rows)
+
+
+def scatter_kernel(ny, nz, part_ref, out_ref, stage, z_send, z_recv, send_sems, recv_sems, z_sems):
+    k, rows, width = out_ref.shape
+    pair = nz * width
+    ty, tz = lax.axis_index("ty"), lax.axis_index("tz")
+    partner_z = 1 - tz
+    section = lax.axis_index("section")
+    chunk = 32
+
+    def device(y, z):
+        return (section, y, z)
+
+    barrier = pltpu.get_barrier_semaphore()
+    pl.semaphore_signal(barrier, inc=1, device_id=device(ty, partner_z), device_id_type=MESH_ID)
+    for step in range(1, ny):
+        pl.semaphore_signal(
+            barrier, inc=1, device_id=device(lax.rem(ty + step, ny), tz), device_id_type=MESH_ID
+        )
+    pl.semaphore_wait(barrier, ny)
+
+    sends = []
+    for step in range(1, ny):
+        peer = lax.rem(ty + step, ny)
+        copy = pltpu.make_async_remote_copy(
+            src_ref=part_ref.at[:, :, pl.ds(pl.multiple_of(peer * pair, pair), pair)],
+            dst_ref=stage.at[ny - step - 1],
+            send_sem=send_sems.at[step - 1],
+            recv_sem=recv_sems.at[ny - step - 1],
+            device_id=device(peer, tz),
+            device_id_type=MESH_ID,
+        )
+        copy.start()
+        sends.append(copy)
+    for slot in range(ny - 1):
+        pltpu.make_async_remote_copy(
+            src_ref=stage.at[slot],
+            dst_ref=stage.at[slot],
+            send_sem=send_sems.at[0],
+            recv_sem=recv_sems.at[slot],
+            device_id=device(ty, partner_z),
+            device_id_type=MESH_ID,
+        ).wait_recv()
+
+    def add_terms(z, target):
+        own = pl.multiple_of((ty * nz + z) * width, width)
+        inside = pl.multiple_of(z * width, width)
+
+        def body(step, carry):
+            plane = step // (rows // chunk)
+            row = pl.multiple_of((step % (rows // chunk)) * chunk, chunk)
+            total = part_ref[plane, pl.ds(row, chunk), pl.ds(own, width)].astype(jnp.float32)
+            for slot in range(ny - 1):
+                total += stage[slot, plane, pl.ds(row, chunk), pl.ds(inside, width)].astype(
+                    jnp.float32
+                )
+            target(plane, row, total)
+            return carry
+
+        lax.fori_loop(0, k * (rows // chunk), body, 0)
+
+    def to_send(plane, row, total):
+        z_send[plane, pl.ds(row, chunk), :] = total
+
+    add_terms(partner_z, to_send)
+    z_copy = pltpu.make_async_remote_copy(
+        src_ref=z_send,
+        dst_ref=z_recv,
+        send_sem=z_sems.at[0],
+        recv_sem=z_sems.at[1],
+        device_id=device(ty, partner_z),
+        device_id_type=MESH_ID,
+    )
+    z_copy.start()
+
+    def to_out(plane, row, total):
+        out_ref[plane, pl.ds(row, chunk), :] = total
+
+    add_terms(tz, to_out)
+    z_copy.wait_recv()
+    out_ref[...] += z_recv[...]
+    z_copy.wait_send()
+    for copy in sends:
+        copy.wait_send()
+
+
+def reduce_columns(partial_rows, collective):
+    k, rows, full = partial_rows.shape
+    ny, nz = lax.axis_size("ty"), lax.axis_size("tz")
+    width = full // (ny * nz)
+    terms = partial_rows.astype(jnp.bfloat16)
+    moved = terms.size * 2
+    return pl.pallas_call(
+        functools.partial(scatter_kernel, ny, nz),
+        out_shape=jax.ShapeDtypeStruct((k, rows, width), jnp.float32),
+        in_specs=[pl.BlockSpec(memory_space=pltpu.VMEM)],
+        out_specs=pl.BlockSpec(memory_space=pltpu.VMEM),
+        scratch_shapes=[
+            pltpu.VMEM((ny - 1, k, rows, nz * width), jnp.bfloat16),
+            pltpu.VMEM((k, rows, width), jnp.float32),
+            pltpu.VMEM((k, rows, width), jnp.float32),
+            pltpu.SemaphoreType.DMA((ny - 1,)),
+            pltpu.SemaphoreType.DMA((ny - 1,)),
+            pltpu.SemaphoreType.DMA((2,)),
+        ],
+        compiler_params=pltpu.CompilerParams(
+            collective_id=collective, has_side_effects=True, vmem_limit_bytes=56 * 1024 * 1024
+        ),
+        cost_estimate=pl.CostEstimate(flops=terms.size, transcendentals=0, bytes_accessed=moved),
+    )(terms)
 
 
 def row_sums(values):
-    return lax.psum(values, "tensor")
+    return lax.psum(values, TENSOR)
 
 
 def layer_core(full_rows, gain_row, up_matrix, down_matrix):
@@ -51,11 +271,7 @@
     return jnp.dot(activated, down_matrix, preferred_element_type=jnp.float32)
 
 
-def layer_backward(saved_rows, cotangent, gain_row, up_matrix, down_matrix):
-    saved_full, cotangent_full = (
-        lax.all_gather(saved_rows, "tensor", axis=1, tiled=True),
-        lax.all_gather(cotangent, "tensor", axis=1, tiled=True),
-    )
+def backward_core(saved_full, cotangent_full, gain_row, up_matrix, down_matrix):
     scaled, inverse = unit_rows(saved_full)
     normed = (scaled * gain_row).astype(jnp.bfloat16)
     pre_act = jnp.dot(normed, up_matrix, preferred_element_type=jnp.float32)
@@ -67,9 +283,12 @@
     norm_partial = lax.dot_general(
         pre_grad, up_matrix, (((1,), (1,)), ((), ())), preferred_element_type=jnp.float32
     )
-    norm_grad = reduce_columns(norm_partial)
+    return norm_partial, scaled, inverse
+
+
+def backward_finish(cotangent, norm_grad, scaled, inverse, gain_row):
     local_width = cotangent.shape[1]
-    full_width = saved_full.shape[1]
+    full_width = scaled.shape[1]
     scaled_cols = column_slice(scaled, local_width)
     gain_cols = lax.dynamic_slice_in_dim(gain_row, column_start(local_width), local_width, 0)
     row_total = row_sums(jnp.sum(scaled_cols * gain_cols * norm_grad, axis=1))
@@ -77,7 +296,6 @@
         gain_cols * norm_grad - scaled_cols * row_total[:, None] / full_width
     )
     return result.astype(jnp.bfloat16)
-
 
 def soft_min(first, second):
     return 0.5 * (
@@ -132,7 +350,7 @@
     ) * keep_mask.astype(jnp.float32)
     counts = jnp.sum(weights, axis=1)
     local_width = final_rows.shape[1]
-    full_width = local_width * lax.axis_size("tensor")
+    full_width = local_width * tensor_size()
     tokens = final_rows.astype(jnp.float32).reshape(row_count, keep_mask.shape[1], local_width)
     pooled = (
         jnp.einsum("rt,rtd->rd", weights, tokens, precision=lax.Precision.HIGHEST) / counts[:, None]
@@ -182,46 +400,57 @@
     opening = section_index == 0
     closing = section_index == lax.axis_size("section") - 1
     local_input = forward_input[0]
-    gathered_input = gather_columns(local_input)
+    closing_saved = jnp.where(closing, local_input, saved_last[0])
+    gathered_input = gather_columns(local_input[None], 0)[0]
+    stored = gather_columns(jnp.stack([saved_first[0], first_cotangent[0], closing_saved]), 1)
     last_partial = layer_core(gathered_input, last_gain[0], last_up[0], last_down[0])
-    hidden_local = (local_input.astype(jnp.float32) + reduce_columns(last_partial)).astype(
-        jnp.bfloat16
+    first_norm_partial, first_scaled, first_inverse = backward_core(
+        stored[0], stored[1], first_gain[0], first_up[0], first_down[0]
+    )
+    reduced = reduce_columns(jnp.stack([last_partial, first_norm_partial]), 3)
+    hidden_local = (local_input.astype(jnp.float32) + reduced[0]).astype(jnp.bfloat16)
+    first_grad = backward_finish(
+        first_cotangent[0], reduced[1], first_scaled, first_inverse, first_gain[0]
     )
     arrived_local = shifted(hidden_local, "section", 1)
-    entry_local = jnp.where(opening, section_entry, arrived_local)
-    entry_full = gather_columns(entry_local)
-    first_partial = layer_core(entry_full, first_gain[0], first_up[0], first_down[0])
-    layer_output = (entry_local.astype(jnp.float32) + reduce_columns(first_partial)).astype(
-        jnp.bfloat16
-    )
-    first_grad = layer_backward(
-        saved_first[0], first_cotangent[0], first_gain[0], first_up[0], first_down[0]
-    )
     returned = shifted(first_grad, "section", -1)
     head_grad = head_cotangent(
         hidden_local, head_gain, head_weight, head_bias, prompt_length, keep_mask, target_box
     )
+    entry_local = jnp.where(opening, section_entry, arrived_local)
     cotangent = jnp.where(closing, head_grad, returned)
-    saved_rows = jnp.where(closing, local_input, saved_last[0])
-    input_gradient = layer_backward(saved_rows, cotangent, last_gain[0], last_up[0], last_down[0])
+    arrived = gather_columns(jnp.stack([entry_local, cotangent]), 2)
+    first_partial = layer_core(arrived[0], first_gain[0], first_up[0], first_down[0])
+    last_norm_partial, last_scaled, last_inverse = backward_core(
+        stored[2], arrived[1], last_gain[0], last_up[0], last_down[0]
+    )
+    reduced_late = reduce_columns(jnp.stack([first_partial, last_norm_partial]), 4)
+    layer_output = (entry_local.astype(jnp.float32) + reduced_late[0]).astype(jnp.bfloat16)
+    input_gradient = backward_finish(
+        cotangent, reduced_late[1], last_scaled, last_inverse, last_gain[0]
+    )
     return (layer_output[None], input_gradient[None])
 
 
 def solution(mesh):
+    sections = mesh.shape["section"]
+    tensors = mesh.shape["tensor"]
+    split = Mesh(mesh.devices.reshape(sections, tensors // 2, 2), ("section", "ty", "tz"))
+    rows = P("section", None, TENSOR)
     placed = (
-        P("section", None, "tensor"),
-        P("section", None, "tensor"),
-        P("section", None, "tensor"),
-        P("section", None, "tensor"),
-        P(None, "tensor"),
+        rows,
+        rows,
+        rows,
+        rows,
+        P(None, TENSOR),
         P("section", None),
-        P("section", None, "tensor"),
-        P("section", "tensor", None),
+        rows,
+        P("section", TENSOR, None),
         P("section", None),
-        P("section", None, "tensor"),
-        P("section", "tensor", None),
+        rows,
+        P("section", TENSOR, None),
         P(),
-        P("tensor", None),
+        P(TENSOR, None),
         P(),
         P(),
         P(),
@@ -229,8 +458,8 @@
     )
     return jax.shard_map(
         per_device,
-        mesh=mesh,
+        mesh=split,
         in_specs=placed,
-        out_specs=(P("section", None, "tensor"), P("section", None, "tensor")),
+        out_specs=(rows, rows),
         check_vma=False,
     )

time: 1170 us -> 870 us (0.74)
  waiting for transfers between devices: 946 us -> 0.56 us
  Pallas kernels: 0 us -> 649 us
  between operations: 30.4 us -> 17.1 us
    pallas_call x0 -> x5, Pallas kernels: none -> 649 us  [the longest x2 342 us: reduce_columns(): pl.pallas_call(functools.partial(scatter_kernel, ny, nz), out_shape=jax.S...]
    all_gather x6 -> x0, waiting for transfers between devices: 552 us -> none  [the longest x2 205 us: gather_columns(): return lax.all_gather(local_rows, 'tensor', axis=1, tiled=True)]
    reduce_scatter x4 -> x0, waiting for transfers between devices: 381 us -> none  [reduce_columns(): lax.psum_scatter(partial_rows.astype(jnp.bfloat16), 'tensor', scatter_dim...]
    another operation x0 -> x6, other arithmetic: none -> 18.5 us  [the longest x1 7.45 us: per_device(): jnp.stack([first_partial, last_norm_partial])]
    mul x2 -> x0, other arithmetic: 13.4 us -> none  [unit_rows(): return (values * inverse, inverse)]
    convert_element_type x2 -> x3, other arithmetic: 2.98 us -> 15.5 us  [the longest x1 11.5 us: unit_rows(): values = values.astype(jnp.float32)]
  transfers between devices with their start and end apart: 12 -> 2, of which waited for: 12 -> 1; matrix products, arithmetic and copies ran while one was open for 7% -> 4% of each run, Pallas kernels for 0% -> 0%
where the time goes in v1:
time: 870 us; the launch traced here: 866 us
  Pallas kernels  649 us (75%)
  blocking collectives  87.8 us (10%)
  other arithmetic  59.1 us (7%)
  matrix products  42.8 us (5%)
  between operations  17.1 us (2%)
    pallas_call x2, Pallas kernels, reduce_columns(): pl.pallas_call(functools.partial(scatter_kernel, ny, nz), out_shape=jax.S...  342 us
    pallas_call x3, Pallas kernels, gather_columns(): pl.pallas_call(functools.partial(gather_kernel, ny, nz), out_shape=jax.Sh...  307 us
    psum x3, blocking collectives, row_sums(): return lax.psum(values, TENSOR)  87.8 us
    dot_general x2, matrix products, backward_core(): lax.dot_general(pre_grad, up_matrix, (((1,), (1,)), ((), ())), preferred_...  19.3 us
  transfers between devices with their start and end apart: 2, of which 1 were waited for; matrix products, arithmetic and copies ran while one was open for 4% of the time, Pallas kernels for 0%

profile of v1, /device:TPU:38, one launch (start us, length us, event | category | flops | bytes accessed | tf_op | source)
XLA Modules:
  0.0 866.4 jit_solution(7021972226236675793)
XLA Ops:
  0.7 1.2 copy-done.3
  1.8 56.1 %shard_map.176 = bf16[1,256,8192]{2,1,0:T(8,128)(2,1)S(1)} custom-call(bf16[1,256,1024]{2,1,0:T(8,128)(2,1)S(1)} %copy-done.3), custom_call_target="tpu_custom_call" | custom-call | bytes 3670016 | tf_op jit(solution)/shard_map/pallas_call | solution.py:135
  57.9 1.9 copy-done.1
  59.9 1.1 broadcast_select_fusion
  61.0 1.2 pad_maximum_fusion.2.x_ref
  62.2 146.2 %shard_map.177 = bf16[3,256,8192]{2,1,0:T(8,128)(2,1)} custom-call(bf16[3,256,1024]{2,1,0:T(8,128)(2,1)S(1)} %pad_maximum_fusion.2.x_ref), custom_call_target="tpu_custom_call" | custom-call | bytes 11010048 | tf_op jit(solution)/shard_map/pallas_call | solution.py:135
  208.4 4.5 multiply_reduce_fusion
  213.1 0.9 fusion.4
  214.0 0.6 copy-done.5
  214.6 3.6 fusion.21
  218.2 10.0 %fusion.1 = bf16[1,256,8192]{2,1,0:T(8,128)(2,1)} fusion(bf16[1,8192,128]{2,1,0:T(8,128)(2,1)} %param.26, bf16[1,128,8192]{2,1,0:T(8,128)(2,1)} %param.27, bf16[3,256,8192]{2,1,0:T(8,128)(2,1)} %shard_map.177, f32[256,128]{1,0:T(8,128)S(1)} %fusion.21), kind=kOutput, calls=%fused_computation.13 | convolution fusion | flops 1076133888 | bytes 12713984 | tf_op jit(solution)/shard_map/dot_general | solution.py:283
  228.2 7.4 fusion
  235.6 7.4 pad_maximum_fusion.part_ref
  243.0 189.5 %shard_map.178 = f32[2,256,1024]{2,1,0:T(8,128)} custom-call(bf16[2,256,8192]{2,1,0:T(8,128)(2,1)} %pad_maximum_fusion.part_ref), custom_call_target="tpu_custom_call" | custom-call | flops 4194304 | bytes 8388608 | tf_op jit(solution)/shard_map/pallas_call | solution.py:241
  432.6 1.4 fusion.101
  434.0 2.2 collective-permute-start
  436.2 11.5 %convert_bitcast_fusion = (f32[256,8192]{1,0:T(8,128)}, f32[256,8192]{1,0:T(8,128)}) fusion(bf16[3,256,8192]{2,1,0:T(8,128)(2,1)} %shard_map.177), kind=kLoop, calls=%fused_computation | loop fusion | flops 4194304 | bytes 25165824 | tf_op jit(solution)/shard_map/convert_element_type | solution.py:32
  448.4 0.7 fusion.166
  449.1 0.3 fusion.142
  449.4 2.0 dynamic-slice_multiply_fusion.2
  451.4 0.1 fusion.170
  451.5 0.8 pad_maximum_fusion.4
  452.3 27.1 %psum.28 = f32[1,5]{1,0:T(1,128)S(1)} all-reduce(f32[1,5]{1,0:T(1,128)S(1)} %pad_maximum_fusion.4), channel_id=1, replica_groups=mesh['section'=32,'ty'=4,'tz'=2] {'ty','tz'}, use_global_device_ids=true, to_apply=%region_4.5 | all-reduce | flops 5 | bytes 40 | tf_op jit(solution)/shard_map/psum | solution.py:262
  479.4 0.6 slice.68
  480.7 0.7 fusion.169
  481.4 0.7 fusion.168
  496.9 0.2 fusion.145
  497.1 2.0 multiply_reduce_fusion.2
  499.1 1.8 fusion.92
  500.9 32.5 %all-reduce.4 = (f32[256]{0:T(256)S(1)}, f32[]{:T(128)}) all-reduce(f32[256]{0:T(256)S(1)} %fusion.92, f32[]{:T(128)} %multiply_reduce_fusion.2), channel_id=1, replica_groups=mesh['section'=32,'ty'=4,'tz'=2] {'ty','tz'}, use_global_device_ids=true, to_apply=%region_8.9 | all-reduce | flops 257 | bytes 2056 | tf_op jit(solution)/shard_map/psum | solution.py:262
  533.4 2.7 fusion.83
  536.1 1.9 collective-permute-start.1
  538.1 3.7 fusion.15
  541.7 0.7 broadcast_divide_fusion.1
  542.5 2.0 subtract_multiply_fusion
  544.5 0.6 collective-permute-done.1
  545.0 1.2 fusion.106
  546.3 1.1 fusion.105
  547.4 0.1 pad_maximum_fusion.3.x_ref
  547.5 104.5 %shard_map.179 = bf16[2,256,8192]{2,1,0:T(8,128)(2,1)} custom-call(bf16[2,256,1024]{2,1,0:T(8,128)(2,1)S(1)} %pad_maximum_fusion.3.x_ref), custom_call_target="tpu_custom_call" | custom-call | bytes 7340032 | tf_op jit(solution)/shard_map/pallas_call | solution.py:135
  652.0 3.1 fusion.9
  655.1 9.4 %fusion.3 = bf16[1,256,8192]{2,1,0:T(8,128)(2,1)} fusion(bf16[1,8192,128]{2,1,0:T(8,128)(2,1)S(1)} %copy-done, bf16[1,128,8192]{2,1,0:T(8,128)(2,1)} %param.24, bf16[2,256,8192]{2,1,0:T(8,128)(2,1)} %shard_map.179, f32[256,128]{1,0:T(8,128)S(1)} %fusion.15), kind=kOutput, calls=%fused_computation.15 | convolution fusion | flops 1076133888 | bytes 12713984 | tf_op jit(solution)/shard_map/dot_general | solution.py:283
  664.5 8.0 fusion.2
  672.5 7.5 pad_maximum_fusion.1.part_ref
  680.0 152.8 %shard_map.180 = f32[2,256,1024]{2,1,0:T(8,128)} custom-call(bf16[2,256,8192]{2,1,0:T(8,128)(2,1)} %pad_maximum_fusion.1.part_ref), custom_call_target="tpu_custom_call" | custom-call | flops 4194304 | bytes 8388608 | tf_op jit(solution)/shard_map/pallas_call | solution.py:241
  832.8 1.8 fusion.88
  834.6 28.2 %psum.31 = f32[256]{0:T(256)S(1)} all-reduce(f32[256]{0:T(256)S(1)} %fusion.88), channel_id=1, replica_groups=mesh['section'=32,'ty'=4,'tz'=2] {'ty','tz'}, use_global_device_ids=true, to_apply=%region_12.13 | all-reduce | flops 256 | bytes 2048 | tf_op jit(solution)/shard_map/psum | solution.py:262
  862.8 3.6 fusion.104
  (36 shorter events, 0.2 us)
Async XLA Ops:
  0.6 227.6 %copy-start = (bf16[1,8192,128]{2,1,0:T(8,128)(2,1)S(1)}, bf16[1,8192,128]{2,1,0:T(8,128)(2,1)}, u32[]{:S(2)}) copy-start(bf16[1,8192,128]{2,1,0:T(8,128)(2,1)} %param.23) | copy-start | bytes 6291460
  0.7 1.2 copy-start.3
  1.8 58.1 %copy-start.4 = (bf16[1,256,1024]{2,1,0:T(8,128)(2,1)S(1)}, bf16[1,256,1024]{2,1,0:T(8,128)(2,1)}, u32[]{:S(2)}) copy-start(bf16[1,256,1024]{2,1,0:T(8,128)(2,1)} %x_ref.1) | copy-start | bytes 1572868
  1.8 59.2 %copy-start.6 = (bf16[1,256,1024]{2,1,0:T(8,128)(2,1)S(1)}, bf16[1,256,1024]{2,1,0:T(8,128)(2,1)}, u32[]{:S(2)}) copy-start(bf16[1,256,1024]{2,1,0:T(8,128)(2,1)} %param.20) | copy-start | bytes 1572868
  57.9 2.0 copy-start.1
  208.4 4.7 copy-start.2
  213.0 1.6 copy-start.5
  213.0 1.6 copy-start.13
  218.2 10.0 %copy-start.9 = (f32[1,8192]{1,0:T(1,128)S(1)}, f32[1,8192]{1,0:T(1,128)}, u32[]{:S(2)}) copy-start(f32[1,8192]{1,0:T(1,128)} %param.22) | copy-start | bytes 98308
  433.9 14.5 %copy-start.11 = (s32[1,256]{1,0:T(1,128)S(1)}, s32[1,256]{1,0:T(1,128)}, u32[]{:S(2)}) copy-start(s32[1,256]{1,0:T(1,128)} %param.32) | copy-start | bytes 3076
  434.0 17.4 %copy-start.10 = (f32[1024,4]{0,1:T(4,128)S(1)}, f32[1024,4]{0,1:T(4,128)}, u32[]{:S(2)}) copy-start(f32[1024,4]{0,1:T(4,128)} %param.29) | copy-start | bytes 49156
  434.0 46.7 %copy-start.12 = (f32[4]{0:T(128)S(1)}, f32[4]{0:T(128)}, u32[]{:S(2)}) copy-start(f32[4]{0:T(128)} %param.30) | copy-start | bytes 52
  434.0 47.4 %copy-start.14 = (s32[1,4]{1,0:T(1,128)S(1)}, s32[1,4]{1,0:T(1,128)}, u32[]{:S(2)}) copy-start(s32[1,4]{1,0:T(1,128)} %param.33) | copy-start | bytes 52
  434.0 99.5 %copy-start.7 = (bf16[1,256,1024]{2,1,0:T(8,128)(2,1)S(1)}, bf16[1,256,1024]{2,1,0:T(8,128)(2,1)}, u32[]{:S(2)}) copy-start(bf16[1,256,1024]{2,1,0:T(8,128)(2,1)} %param.20) | copy-start | bytes 1572868
  434.0 112.3 %collective-permute-start = (bf16[256,1024]{1,0:T(8,128)(2,1)S(1)}, bf16[256,1024]{1,0:T(8,128)(2,1)}, u32[]{:S(2)}, u32[]{:S(2)}) collective-permute-start(bf16[256,1024]{1,0:T(8,128)(2,1)S(1)} %fusion.101), channel_id=1, source_target_pairs={{0,8},{8,16},{16,24},{24,32},{32,40},{40,48},{48,56},{56,64},{64,7... | collective-permute-start | bytes 1572872 | tf_op jit(solution)/shard_map/ppermute | solution.py:20
  536.1 8.9 %collective-permute-start.1 = (bf16[256,1024]{1,0:T(8,128)(2,1)}, bf16[256,1024]{1,0:T(8,128)(2,1)}, u32[]{:S(2)}, u32[]{:S(2)}) collective-permute-start(bf16[256,1024]{1,0:T(8,128)(2,1)} %fusion.83), channel_id=1, source_target_pairs={{8,0},{16,8},{24,16},{32,24},{40,32},{48,40},{56,48},{64,56},{72,6... | collective-permute-start | bytes 1572872 | tf_op jit(solution)/shard_map/ppermute | solution.py:20
  538.1 8.2 copy-start.8

commit v2 on v1

--- a/solution.py
+++ b/solution.py
@@ -258,8 +258,68 @@
     )(terms)
 
 
-def row_sums(values):
-    return lax.psum(values, TENSOR)
+def sum_kernel(ny, nz, v_ref, out_ref, slots, send_sems, recv_sems):
+    ty, tz = lax.axis_index("ty"), lax.axis_index("tz")
+    me = ty * nz + tz
+    section = lax.axis_index("section")
+    peers = [(lax.rem(ty + dy, ny), lax.rem(tz + dz, nz)) for dy in range(ny) for dz in range(nz)][1:]
+
+    barrier = pltpu.get_barrier_semaphore()
+    for y, z in peers:
+        pl.semaphore_signal(barrier, inc=1, device_id=(section, y, z), device_id_type=MESH_ID)
+    pl.semaphore_wait(barrier, len(peers))
+    sends = []
+    for number, (y, z) in enumerate(peers):
+        copy = pltpu.make_async_remote_copy(
+            src_ref=v_ref,
+            dst_ref=slots.at[me],
+            send_sem=send_sems.at[number],
+            recv_sem=recv_sems.at[me],
+            device_id=(section, y, z),
+            device_id_type=MESH_ID,
+        )
+        copy.start()
+        sends.append(copy)
+    slots[me] = v_ref[...]
+    for y, z in peers:
+        source = y * nz + z
+        pltpu.make_async_remote_copy(
+            src_ref=v_ref,
+            dst_ref=slots.at[source],
+            send_sem=send_sems.at[0],
+            recv_sem=recv_sems.at[source],
+            device_id=(section, y, z),
+            device_id_type=MESH_ID,
+        ).wait_recv()
+    total = slots[0]
+    for source in range(1, ny * nz):
+        total = total + slots[source]
+    out_ref[...] = total
+    for copy in sends:
+        copy.wait_send()
+
+
+def row_sums(values, collective):
+    shape = values.shape
+    flat = values.reshape(-1).astype(jnp.float32)
+    lanes = 128
+    padded = -(-flat.shape[0] // lanes) * lanes
+    rows = jnp.pad(flat, (0, padded - flat.shape[0])).reshape(padded // lanes, lanes)
+    ny, nz = lax.axis_size("ty"), lax.axis_size("tz")
+    summed = pl.pallas_call(
+        functools.partial(sum_kernel, ny, nz),
+        out_shape=jax.ShapeDtypeStruct(rows.shape, jnp.float32),
+        in_specs=[pl.BlockSpec(memory_space=pltpu.VMEM)],
+        out_specs=pl.BlockSpec(memory_space=pltpu.VMEM),
+        scratch_shapes=[
+            pltpu.VMEM((ny * nz,) + rows.shape, jnp.float32),
+            pltpu.SemaphoreType.DMA((ny * nz - 1,)),
+            pltpu.SemaphoreType.DMA((ny * nz,)),
+        ],
+        compiler_params=pltpu.CompilerParams(collective_id=collective, has_side_effects=True),
+        cost_estimate=pl.CostEstimate(flops=rows.size * 8, transcendentals=0, bytes_accessed=rows.size * 64),
+    )(rows)
+    return summed.reshape(-1)[: flat.shape[0]].reshape(shape)
 
 
 def layer_core(full_rows, gain_row, up_matrix, down_matrix):
@@ -286,12 +346,12 @@
     return norm_partial, scaled, inverse
 
 
-def backward_finish(cotangent, norm_grad, scaled, inverse, gain_row):
+def backward_finish(cotangent, norm_grad, scaled, inverse, gain_row, collective):
     local_width = cotangent.shape[1]
     full_width = scaled.shape[1]
     scaled_cols = column_slice(scaled, local_width)
     gain_cols = lax.dynamic_slice_in_dim(gain_row, column_start(local_width), local_width, 0)
-    row_total = row_sums(jnp.sum(scaled_cols * gain_cols * norm_grad, axis=1))
+    row_total = row_sums(jnp.sum(scaled_cols * gain_cols * norm_grad, axis=1), collective)
     result = cotangent.astype(jnp.float32) + inverse * (
         gain_cols * norm_grad - scaled_cols * row_total[:, None] / full_width
     )
@@ -358,7 +418,7 @@
     gain_cols = lax.dynamic_slice_in_dim(head_gain, column_start(local_width), local_width, 0)
     logit_part = jnp.dot(pooled * gain_cols, head_weight, precision=lax.Precision.HIGHEST)
     square_part = jnp.sum(pooled * pooled, axis=1, keepdims=True)
-    totals = row_sums(jnp.concatenate([logit_part, square_part], axis=1))
+    totals = row_sums(jnp.concatenate([logit_part, square_part], axis=1), 5)
     inverse = lax.rsqrt(totals[:, 4] / full_width + epsilon)
     logits = totals[:, :4] * inverse[:, None] + head_bias
 
@@ -369,7 +429,7 @@
     logit_grad = pullback(jnp.ones((), jnp.float32))[0]
     scaled_grad = jnp.dot(logit_grad, head_weight.T, precision=lax.Precision.HIGHEST)
     unit_pooled = pooled * inverse[:, None]
-    row_total = row_sums(jnp.sum(unit_pooled * gain_cols * scaled_grad, axis=1))
+    row_total = row_sums(jnp.sum(unit_pooled * gain_cols * scaled_grad, axis=1), 6)
     pooled_grad = inverse[:, None] * (
         gain_cols * scaled_grad - unit_pooled * row_total[:, None] / full_width
     )
@@ -410,7 +470,7 @@
     reduced = reduce_columns(jnp.stack([last_partial, first_norm_partial]), 3)
     hidden_local = (local_input.astype(jnp.float32) + reduced[0]).astype(jnp.bfloat16)
     first_grad = backward_finish(
-        first_cotangent[0], reduced[1], first_scaled, first_inverse, first_gain[0]
+        first_cotangent[0], reduced[1], first_scaled, first_inverse, first_gain[0], 7
     )
     arrived_local = shifted(hidden_local, "section", 1)
     returned = shifted(first_grad, "section", -1)
@@ -427,7 +487,7 @@
     reduced_late = reduce_columns(jnp.stack([first_partial, last_norm_partial]), 4)
     layer_output = (entry_local.astype(jnp.float32) + reduced_late[0]).astype(jnp.bfloat16)
     input_gradient = backward_finish(
-        cotangent, reduced_late[1], last_scaled, last_inverse, last_gain[0]
+        cotangent, reduced_late[1], last_scaled, last_inverse, last_gain[0], 8
     )
     return (layer_output[None], input_gradient[None])
 

time: 870 us -> 832 us (0.956); the launches traced: 866 us -> 815 us
  blocking collectives: 87.8 us -> 0 us
  Pallas kernels: 649 us -> 683 us
    psum x3 -> x0, blocking collectives: 87.8 us -> none  [row_sums(): return lax.psum(values, TENSOR)]
    pallas_call x0 -> x4, Pallas kernels: none -> 45.2 us  [row_sums(): pl.pallas_call(functools.partial(sum_kernel, ny, nz), out_shape=jax.Shape...]
  transfers between devices with their start and end apart: 2 -> 2, of which waited for: 1 -> 0; matrix products, arithmetic and copies ran while one was open for 4% -> 4% of each run, Pallas kernels for 0% -> 4%
where the time goes in v2:
time: 832 us; the launch traced here: 815 us
  Pallas kernels  683 us (82%)
  other arithmetic  60.5 us (7%)
  matrix products  42.8 us (5%)
  between operations  16.5 us (2%)
    pallas_call x2, Pallas kernels, reduce_columns(): pl.pallas_call(functools.partial(scatter_kernel, ny, nz), out_shape=jax.S...  339 us
    pallas_call x3, Pallas kernels, gather_columns(): pl.pallas_call(functools.partial(gather_kernel, ny, nz), out_shape=jax.Sh...  299 us
    pallas_call x4, Pallas kernels, row_sums(): pl.pallas_call(functools.partial(sum_kernel, ny, nz), out_shape=jax.Shape...  45.2 us
    dot_general x2, matrix products, backward_core(): lax.dot_general(pre_grad, up_matrix, (((1,), (1,)), ((), ())), preferred_...  19.3 us
  transfers between devices with their start and end apart: 2, of which 0 were waited for; matrix products, arithmetic and copies ran while one was open for 4% of the time, Pallas kernels for 4%

profile of v2, /device:TPU:38, one launch (start us, length us, event | category | flops | bytes accessed | tf_op | source)
XLA Modules:
  0.0 815.3 jit_solution(13684585862832821222)
XLA Ops:
  0.7 1.2 copy-done.3
  1.8 56.1 %shard_map.176 = bf16[1,256,8192]{2,1,0:T(8,128)(2,1)S(1)} custom-call(bf16[1,256,1024]{2,1,0:T(8,128)(2,1)S(1)} %copy-done.3), custom_call_target="tpu_custom_call" | custom-call | bytes 3670016 | tf_op jit(solution)/shard_map/pallas_call | solution.py:135
  57.9 1.9 copy-done.1
  59.9 1.1 broadcast_select_fusion
  61.0 1.2 pad_maximum_fusion.2.x_ref
  62.2 146.2 %shard_map.177 = bf16[3,256,8192]{2,1,0:T(8,128)(2,1)} custom-call(bf16[3,256,1024]{2,1,0:T(8,128)(2,1)S(1)} %pad_maximum_fusion.2.x_ref), custom_call_target="tpu_custom_call" | custom-call | bytes 11010048 | tf_op jit(solution)/shard_map/pallas_call | solution.py:135
  208.4 4.5 multiply_reduce_fusion
  213.1 0.9 fusion.4
  214.0 0.6 copy-done.5
  214.6 3.6 fusion.21
  218.2 10.0 %fusion.1 = bf16[1,256,8192]{2,1,0:T(8,128)(2,1)} fusion(bf16[1,8192,128]{2,1,0:T(8,128)(2,1)} %param.26, bf16[1,128,8192]{2,1,0:T(8,128)(2,1)} %param.27, bf16[3,256,8192]{2,1,0:T(8,128)(2,1)} %shard_map.177, f32[256,128]{1,0:T(8,128)S(1)} %fusion.21), kind=kOutput, calls=%fused_computation.13 | convolution fusion | flops 1076133888 | bytes 12713984 | tf_op jit(solution)/shard_map/dot_general | solution.py:343
  228.2 7.4 fusion
  235.6 7.4 pad_maximum_fusion.part_ref
  243.0 189.5 %shard_map.178 = f32[2,256,1024]{2,1,0:T(8,128)} custom-call(bf16[2,256,8192]{2,1,0:T(8,128)(2,1)} %pad_maximum_fusion.part_ref), custom_call_target="tpu_custom_call" | custom-call | flops 4194304 | bytes 8388608 | tf_op jit(solution)/shard_map/pallas_call | solution.py:241
  432.5 1.4 fusion.101
  433.9 2.2 collective-permute-start
  436.2 11.5 %convert_bitcast_fusion = (f32[256,8192]{1,0:T(8,128)}, f32[256,8192]{1,0:T(8,128)}) fusion(bf16[3,256,8192]{2,1,0:T(8,128)(2,1)} %shard_map.177), kind=kLoop, calls=%fused_computation | loop fusion | flops 4194304 | bytes 25165824 | tf_op jit(solution)/shard_map/convert_element_type | solution.py:32
  447.7 2.4 fusion.92
  450.1 11.3 %shard_map.181 = f32[2,128]{1,0:T(2,128)} custom-call(f32[2,128]{1,0:T(2,128)} %bitcast.225), custom_call_target="tpu_custom_call" | custom-call | flops 2048 | bytes 16384 | tf_op jit(solution)/shard_map/pallas_call | solution.py:309
  461.5 2.7 fusion.83
  464.8 0.6 fusion.166
  465.4 0.3 fusion.142
  465.8 1.9 dynamic-slice_multiply_fusion.2
  467.8 0.8 maximum_bitcast_fusion
  468.6 0.5 pad_bitcast_fusion.1.v_ref
  469.1 2.5 collective-permute-start.1
  471.6 11.3 %shard_map.179 = f32[1,128]{1,0:T(1,128)} custom-call(f32[1,128]{1,0:T(1,128)} %pad_bitcast_fusion.1.v_ref), custom_call_target="tpu_custom_call" | custom-call | flops 1024 | bytes 8192 | tf_op jit(solution)/shard_map/pallas_call | solution.py:309
  483.0 1.2 slice.76
  484.9 0.6 broadcast_multiply_fusion
  485.5 0.7 fusion.169
  486.1 0.6 fusion.168
  501.2 1.9 multiply_reduce_fusion.2
  503.1 1.1 pad_bitcast_fusion.v_ref
  504.2 3.7 fusion.15
  507.9 0.6 broadcast_divide_fusion.1
  508.5 11.3 %shard_map.180 = f32[1,128]{1,0:T(1,128)} custom-call(f32[1,128]{1,0:T(1,128)} %pad_bitcast_fusion.v_ref), custom_call_target="tpu_custom_call" | custom-call | flops 1024 | bytes 8192 | tf_op jit(solution)/shard_map/pallas_call | solution.py:309
  519.8 1.9 subtract_multiply_fusion
  521.7 1.2 fusion.106
  522.9 1.1 fusion.105
  524.2 96.8 %shard_map.182 = bf16[2,256,8192]{2,1,0:T(8,128)(2,1)} custom-call(bf16[2,256,1024]{2,1,0:T(8,128)(2,1)S(1)} %pad_maximum_fusion.3.x_ref), custom_call_target="tpu_custom_call" | custom-call | bytes 7340032 | tf_op jit(solution)/shard_map/pallas_call | solution.py:135
  621.0 3.1 fusion.9
  624.1 9.4 %fusion.3 = bf16[1,256,8192]{2,1,0:T(8,128)(2,1)} fusion(bf16[1,8192,128]{2,1,0:T(8,128)(2,1)S(1)} %copy-done, bf16[1,128,8192]{2,1,0:T(8,128)(2,1)} %param.24, bf16[2,256,8192]{2,1,0:T(8,128)(2,1)} %shard_map.182, f32[256,128]{1,0:T(8,128)S(1)} %fusion.15), kind=kOutput, calls=%fused_computation.15 | convolution fusion | flops 1076133888 | bytes 12713984 | tf_op jit(solution)/shard_map/dot_general | solution.py:343
  633.5 8.0 fusion.2
  641.5 7.5 pad_maximum_fusion.1.part_ref
  649.0 149.1 %shard_map.183 = f32[2,256,1024]{2,1,0:T(8,128)} custom-call(bf16[2,256,8192]{2,1,0:T(8,128)(2,1)} %pad_maximum_fusion.1.part_ref), custom_call_target="tpu_custom_call" | custom-call | flops 4194304 | bytes 8388608 | tf_op jit(solution)/shard_map/pallas_call | solution.py:241
  798.0 2.4 fusion.88
  800.4 11.3 %shard_map.184 = f32[2,128]{1,0:T(2,128)} custom-call(f32[2,128]{1,0:T(2,128)} %bitcast.226), custom_call_target="tpu_custom_call" | custom-call | flops 2048 | bytes 16384 | tf_op jit(solution)/shard_map/pallas_call | solution.py:309
  811.8 3.6 fusion.104
  (39 shorter events, 0.7 us)
Async XLA Ops:
  0.6 227.6 %copy-start = (bf16[1,8192,128]{2,1,0:T(8,128)(2,1)S(1)}, bf16[1,8192,128]{2,1,0:T(8,128)(2,1)}, u32[]{:S(2)}) copy-start(bf16[1,8192,128]{2,1,0:T(8,128)(2,1)} %param.23) | copy-start | bytes 6291460
  0.7 1.2 copy-start.3
  1.8 58.1 %copy-start.4 = (bf16[1,256,1024]{2,1,0:T(8,128)(2,1)S(1)}, bf16[1,256,1024]{2,1,0:T(8,128)(2,1)}, u32[]{:S(2)}) copy-start(bf16[1,256,1024]{2,1,0:T(8,128)(2,1)} %x_ref.1) | copy-start | bytes 1572868
  1.8 59.2 %copy-start.6 = (bf16[1,256,1024]{2,1,0:T(8,128)(2,1)S(1)}, bf16[1,256,1024]{2,1,0:T(8,128)(2,1)}, u32[]{:S(2)}) copy-start(bf16[1,256,1024]{2,1,0:T(8,128)(2,1)} %param.20) | copy-start | bytes 1572868
  57.9 2.0 copy-start.1
  208.4 4.7 copy-start.2
  213.0 1.6 copy-start.5
  213.0 1.6 copy-start.13
  218.2 10.0 %copy-start.9 = (f32[1,8192]{1,0:T(1,128)S(1)}, f32[1,8192]{1,0:T(1,128)}, u32[]{:S(2)}) copy-start(f32[1,8192]{1,0:T(1,128)} %param.22) | copy-start | bytes 98308
  433.9 27.5 %copy-start.7 = (bf16[1,256,1024]{2,1,0:T(8,128)(2,1)S(1)}, bf16[1,256,1024]{2,1,0:T(8,128)(2,1)}, u32[]{:S(2)}) copy-start(bf16[1,256,1024]{2,1,0:T(8,128)(2,1)} %param.20) | copy-start | bytes 1572868
  433.9 89.0 %collective-permute-start = (bf16[256,1024]{1,0:T(8,128)(2,1)S(1)}, bf16[256,1024]{1,0:T(8,128)(2,1)}, u32[]{:S(2)}, u32[]{:S(2)}) collective-permute-start(bf16[256,1024]{1,0:T(8,128)(2,1)S(1)} %fusion.101), channel_id=1, source_target_pairs={{0,8},{8,16},{16,24},{24,32},{32,40},{40,48},{48,56},{56,64},{64,7... | collective-permute-start | bytes 1572872 | tf_op jit(solution)/shard_map/ppermute | solution.py:20
  447.7 17.1 %copy-start.11 = (s32[1,256]{1,0:T(1,128)S(1)}, s32[1,256]{1,0:T(1,128)}, u32[]{:S(2)}) copy-start(s32[1,256]{1,0:T(1,128)} %param.32) | copy-start | bytes 3076
  447.7 20.0 %copy-start.10 = (f32[1024,4]{0,1:T(4,128)S(1)}, f32[1024,4]{0,1:T(4,128)}, u32[]{:S(2)}) copy-start(f32[1024,4]{0,1:T(4,128)} %param.29) | copy-start | bytes 49156
  447.7 37.2 %copy-start.12 = (f32[4]{0:T(128)S(1)}, f32[4]{0:T(128)}, u32[]{:S(2)}) copy-start(f32[4]{0:T(128)} %param.30) | copy-start | bytes 52
  447.7 38.5 %copy-start.14 = (s32[1,4]{1,0:T(1,128)S(1)}, s32[1,4]{1,0:T(1,128)}, u32[]{:S(2)}) copy-start(s32[1,4]{1,0:T(1,128)} %param.33) | copy-start | bytes 52
  469.1 52.6 %collective-permute-start.1 = (bf16[256,1024]{1,0:T(8,128)(2,1)}, bf16[256,1024]{1,0:T(8,128)(2,1)}, u32[]{:S(2)}, u32[]{:S(2)}) collective-permute-start(bf16[256,1024]{1,0:T(8,128)(2,1)} %fusion.83), channel_id=1, source_target_pairs={{8,0},{16,8},{24,16},{32,24},{40,32},{48,40},{56,48},{64,56},{72,6... | collective-permute-start | bytes 1572872 | tf_op jit(solution)/shard_map/ppermute | solution.py:20
  504.2 18.7 %copy-start.8 = (bf16[256,1024]{1,0:T(8,128)(2,1)S(1)}, bf16[256,1024]{1,0:T(8,128)(2,1)}, u32[]{:S(2)}) copy-start(bf16[256,1024]{1,0:T(8,128)(2,1)} %param.21) | copy-start | bytes 1572868

commit v3 on v2

--- a/solution.py
+++ b/solution.py
@@ -232,19 +232,19 @@
         copy.wait_send()
 
 
-def reduce_columns(partial_rows, collective):
+def reduce_columns(partial_rows, collective, term_type=jnp.bfloat16):
     k, rows, full = partial_rows.shape
     ny, nz = lax.axis_size("ty"), lax.axis_size("tz")
     width = full // (ny * nz)
-    terms = partial_rows.astype(jnp.bfloat16)
-    moved = terms.size * 2
+    terms = partial_rows.astype(term_type)
+    moved = terms.size * terms.dtype.itemsize
     return pl.pallas_call(
         functools.partial(scatter_kernel, ny, nz),
         out_shape=jax.ShapeDtypeStruct((k, rows, width), jnp.float32),
         in_specs=[pl.BlockSpec(memory_space=pltpu.VMEM)],
         out_specs=pl.BlockSpec(memory_space=pltpu.VMEM),
         scratch_shapes=[
-            pltpu.VMEM((ny - 1, k, rows, nz * width), jnp.bfloat16),
+            pltpu.VMEM((ny - 1, k, rows, nz * width), term_type),
             pltpu.VMEM((k, rows, width), jnp.float32),
             pltpu.VMEM((k, rows, width), jnp.float32),
             pltpu.SemaphoreType.DMA((ny - 1,)),
@@ -322,40 +322,69 @@
     return summed.reshape(-1)[: flat.shape[0]].reshape(shape)
 
 
-def layer_core(full_rows, gain_row, up_matrix, down_matrix):
-    scaled, inverse = unit_rows(full_rows)
-    normed = (scaled * gain_row).astype(jnp.bfloat16)
-    activated = jax.nn.silu(jnp.dot(normed, up_matrix, preferred_element_type=jnp.float32)).astype(
-        jnp.bfloat16
-    )
-    return jnp.dot(activated, down_matrix, preferred_element_type=jnp.float32)
-
-
-def backward_core(saved_full, cotangent_full, gain_row, up_matrix, down_matrix):
-    scaled, inverse = unit_rows(saved_full)
-    normed = (scaled * gain_row).astype(jnp.bfloat16)
-    pre_act = jnp.dot(normed, up_matrix, preferred_element_type=jnp.float32)
-    act_grad = lax.dot_general(
-        cotangent_full, down_matrix, (((1,), (1,)), ((), ())), preferred_element_type=jnp.float32
-    )
+def spread_weights(up_matrix, down_matrix):
+    n = tensor_size()
+    full, hidden = up_matrix.shape
+    width = full // n
+    up_blocks = lax.all_to_all(up_matrix.reshape(n, width, hidden), TENSOR, 0, 0, tiled=True)
+    up_local = up_blocks.transpose(1, 0, 2).reshape(width, n * hidden)
+    down_blocks = down_matrix.reshape(hidden, n, width).transpose(1, 0, 2)
+    down_local = lax.all_to_all(down_blocks, TENSOR, 0, 0, tiled=True).reshape(n * hidden, width)
+    return up_local, down_local
+
+
+def grouped_sum(left, right, contract):
+    n = tensor_size()
+    rows = left.shape[0]
+    hidden = left.shape[1] // n
+    left_groups = left.reshape(rows, n, hidden)
+    if contract == "rows":
+        right_groups = right.reshape(n, hidden, right.shape[1])
+        terms = jnp.einsum("tgk,gkf->gtf", left_groups, right_groups, preferred_element_type=jnp.float32)
+    else:
+        right_groups = right.reshape(right.shape[0], n, hidden)
+        terms = jnp.einsum("tgk,fgk->gtf", left_groups, right_groups, preferred_element_type=jnp.float32)
+    return jnp.sum(terms.astype(jnp.bfloat16).astype(jnp.float32), axis=0)
+
+
+def normed_rows(local_rows, total_squares, gain_cols, full_width):
+    values = local_rows.astype(jnp.float32)
+    inverse = lax.rsqrt(total_squares[:, None] / full_width + epsilon)
+    scaled = values * inverse
+    return scaled, inverse, (scaled * gain_cols).astype(jnp.bfloat16)
+
+
+def local_squares(local_rows):
+    values = local_rows.astype(jnp.float32)
+    return jnp.sum(values * values, axis=-1)
+
+
+def layer_forward(local_rows, squares, gain_cols, up_local, full_width):
+    scaled, inverse, normed = normed_rows(local_rows, squares, gain_cols, full_width)
+    return jnp.dot(normed, up_local, preferred_element_type=jnp.float32)
+
+
+def layer_back_partials(saved_rows, squares, cotangent, gain_cols, up_local, down_local, full_width):
+    scaled, inverse, normed = normed_rows(saved_rows, squares, gain_cols, full_width)
+    pre_part = jnp.dot(normed, up_local, preferred_element_type=jnp.float32)
+    grad_part = lax.dot_general(
+        cotangent, down_local, (((1,), (1,)), ((), ())), preferred_element_type=jnp.float32
+    )
+    return pre_part, grad_part, scaled, inverse
+
+
+def pre_gradient(pre_act, act_grad):
     sigmoid_pre = jax.nn.sigmoid(pre_act)
-    pre_grad = (act_grad * sigmoid_pre * (1.0 + pre_act * (1.0 - sigmoid_pre))).astype(jnp.bfloat16)
-    norm_partial = lax.dot_general(
-        pre_grad, up_matrix, (((1,), (1,)), ((), ())), preferred_element_type=jnp.float32
-    )
-    return norm_partial, scaled, inverse
-
-
-def backward_finish(cotangent, norm_grad, scaled, inverse, gain_row, collective):
-    local_width = cotangent.shape[1]
-    full_width = scaled.shape[1]
-    scaled_cols = column_slice(scaled, local_width)
-    gain_cols = lax.dynamic_slice_in_dim(gain_row, column_start(local_width), local_width, 0)
-    row_total = row_sums(jnp.sum(scaled_cols * gain_cols * norm_grad, axis=1), collective)
+    return (act_grad * sigmoid_pre * (1.0 + pre_act * (1.0 - sigmoid_pre))).astype(jnp.bfloat16)
+
+
+def back_finish(cotangent, norm_grad, scaled, inverse, gain_cols, full_width, collective):
+    row_total = row_sums(jnp.sum(scaled * gain_cols * norm_grad, axis=1), collective)
     result = cotangent.astype(jnp.float32) + inverse * (
-        gain_cols * norm_grad - scaled_cols * row_total[:, None] / full_width
+        gain_cols * norm_grad - scaled * row_total[:, None] / full_width
     )
     return result.astype(jnp.bfloat16)
+
 
 def soft_min(first, second):
     return 0.5 * (
@@ -460,17 +489,34 @@
     opening = section_index == 0
     closing = section_index == lax.axis_size("section") - 1
     local_input = forward_input[0]
+    width = local_input.shape[1]
+    full_width = width * tensor_size()
+    last_gain_cols = lax.dynamic_slice_in_dim(last_gain[0], column_start(width), width, 0)
+    first_gain_cols = lax.dynamic_slice_in_dim(first_gain[0], column_start(width), width, 0)
+    last_up_local, last_down_local = spread_weights(last_up[0], last_down[0])
+    first_up_local, first_down_local = spread_weights(first_up[0], first_down[0])
     closing_saved = jnp.where(closing, local_input, saved_last[0])
-    gathered_input = gather_columns(local_input[None], 0)[0]
-    stored = gather_columns(jnp.stack([saved_first[0], first_cotangent[0], closing_saved]), 1)
-    last_partial = layer_core(gathered_input, last_gain[0], last_up[0], last_down[0])
-    first_norm_partial, first_scaled, first_inverse = backward_core(
-        stored[0], stored[1], first_gain[0], first_up[0], first_down[0]
-    )
-    reduced = reduce_columns(jnp.stack([last_partial, first_norm_partial]), 3)
-    hidden_local = (local_input.astype(jnp.float32) + reduced[0]).astype(jnp.bfloat16)
-    first_grad = backward_finish(
-        first_cotangent[0], reduced[1], first_scaled, first_inverse, first_gain[0], 7
+    squares = row_sums(
+        jnp.stack(
+            [local_squares(local_input), local_squares(saved_first[0]), local_squares(closing_saved)]
+        ),
+        9,
+    )
+    last_pre = layer_forward(local_input, squares[0], last_gain_cols, last_up_local, full_width)
+    first_pre, first_grad_part, first_scaled, first_inverse = layer_back_partials(
+        saved_first[0], squares[1], first_cotangent[0], first_gain_cols, first_up_local,
+        first_down_local, full_width,
+    )
+    reduced = reduce_columns(jnp.stack([last_pre, first_pre, first_grad_part]), 3, jnp.float32)
+    last_act = jax.nn.silu(reduced[0]).astype(jnp.bfloat16)
+    first_pre_grad = pre_gradient(reduced[1], reduced[2])
+    spread = gather_columns(jnp.stack([last_act, first_pre_grad]), 0)
+    last_out = grouped_sum(spread[0], last_down_local, "rows")
+    hidden_local = (local_input.astype(jnp.float32) + last_out).astype(jnp.bfloat16)
+    first_norm_grad = grouped_sum(spread[1], first_up_local, "cols")
+    first_grad = back_finish(
+        first_cotangent[0], first_norm_grad, first_scaled, first_inverse, first_gain_cols,
+        full_width, 7,
     )
     arrived_local = shifted(hidden_local, "section", 1)
     returned = shifted(first_grad, "section", -1)
@@ -479,15 +525,23 @@
     )
     entry_local = jnp.where(opening, section_entry, arrived_local)
     cotangent = jnp.where(closing, head_grad, returned)
-    arrived = gather_columns(jnp.stack([entry_local, cotangent]), 2)
-    first_partial = layer_core(arrived[0], first_gain[0], first_up[0], first_down[0])
-    last_norm_partial, last_scaled, last_inverse = backward_core(
-        stored[2], arrived[1], last_gain[0], last_up[0], last_down[0]
-    )
-    reduced_late = reduce_columns(jnp.stack([first_partial, last_norm_partial]), 4)
-    layer_output = (entry_local.astype(jnp.float32) + reduced_late[0]).astype(jnp.bfloat16)
-    input_gradient = backward_finish(
-        cotangent, reduced_late[1], last_scaled, last_inverse, last_gain[0], 8
+    entry_squares = row_sums(local_squares(entry_local), 10)
+    first_pre_late = layer_forward(entry_local, entry_squares, first_gain_cols, first_up_local, full_width)
+    last_pre_late, last_grad_part, last_scaled, last_inverse = layer_back_partials(
+        closing_saved, squares[2], cotangent, last_gain_cols, last_up_local, last_down_local,
+        full_width,
+    )
+    reduced_late = reduce_columns(
+        jnp.stack([first_pre_late, last_pre_late, last_grad_part]), 4, jnp.float32
+    )
+    first_act = jax.nn.silu(reduced_late[0]).astype(jnp.bfloat16)
+    last_pre_grad = pre_gradient(reduced_late[1], reduced_late[2])
+    spread_late = gather_columns(jnp.stack([first_act, last_pre_grad]), 1)
+    first_out = grouped_sum(spread_late[0], first_down_local, "rows")
+    layer_output = (entry_local.astype(jnp.float32) + first_out).astype(jnp.bfloat16)
+    last_norm_grad = grouped_sum(spread_late[1], last_up_local, "cols")
+    input_gradient = back_finish(
+        cotangent, last_norm_grad, last_scaled, last_inverse, last_gain_cols, full_width, 8
     )
     return (layer_output[None], input_gradient[None])
 

time: 832 us -> 520 us (0.62); the launches traced: 815 us -> 518 us
  Pallas kernels: 683 us -> 265 us
  waiting for transfers between devices: 0.01 us -> 66.8 us
  blocking collectives: 0 us -> 63.7 us
  other arithmetic: 60.5 us -> 27.7 us
  local copies, waits for them, and re-layouts: 7.94 us -> 38.8 us
  matrix products: 42.8 us -> 20 us
  starting transfers between devices: 4.77 us -> 18.8 us
    pallas_call x3 -> x2, Pallas kernels: 299 us -> 46.6 us  [gather_columns(): pl.pallas_call(functools.partial(gather_kernel, ny, nz), out_shape=jax.Sh...]
    pallas_call x2, Pallas kernels: 339 us -> 109 us  [reduce_columns(): pl.pallas_call(functools.partial(scatter_kernel, ny, nz), out_shape=jax.S...]
    all_to_all x0 -> x3, waiting for transfers between devices: none -> 66.7 us  [the longest x1 33.5 us: spread_weights(): lax.all_to_all(up_matrix.reshape(n, width, hidden), TENSOR, 0, 0, tiled=T...]
    pallas_call x4 -> x6, Pallas kernels: 45.2 us -> 109 us  [row_sums(): pl.pallas_call(functools.partial(sum_kernel, ny, nz), out_shape=jax.Shape...]
    all_to_all x0 -> x1, blocking collectives: none -> 63.7 us  [spread_weights(): lax.all_to_all(up_matrix.reshape(n, width, hidden), TENSOR, 0, 0, tiled=T...]
    dot_general x6 -> x10, matrix products: 42.1 us -> 19.2 us  [the longest x2 5.15 us: layer_back_partials(): lax.dot_general(cotangent, down_local, (((1,), (1,)), ((), ())), preferre...]
    unnamed x30 -> x48, local copies, waits for them, and re-layouts: 3.85 us -> 18.7 us
    all_to_all x0 -> x3, starting transfers between devices: none -> 14.6 us  [the longest x2 11 us: spread_weights(): lax.all_to_all(down_blocks, TENSOR, 0, 0, tiled=True)]
  transfers between devices with their start and end apart: 2 -> 5, of which waited for: 0 -> 2; matrix products, arithmetic and copies ran while one was open for 4% -> 11% of each run, Pallas kernels for 4% -> 31%
where the time goes in v3:
time: 520 us; the launch traced here: 518 us
  Pallas kernels  265 us (51%)
  waiting for transfers between devices  66.8 us (13%)
  blocking collectives  63.7 us (12%)
  local copies, waits for them, and re-layouts  38.8 us (7%)
  other arithmetic  27.7 us (5%)
  matrix products  20 us (4%)
  starting transfers between devices  18.8 us (4%)
  between operations  16.9 us (3%)
    pallas_call x6, Pallas kernels, row_sums(): pl.pallas_call(functools.partial(sum_kernel, ny, nz), out_shape=jax.Shape...  109 us
    pallas_call x2, Pallas kernels, reduce_columns(): pl.pallas_call(functools.partial(scatter_kernel, ny, nz), out_shape=jax.S...  109 us
    all_to_all x1, blocking collectives, spread_weights(): lax.all_to_all(up_matrix.reshape(n, width, hidden), TENSOR, 0, 0, tiled=T...  63.7 us
    pallas_call x2, Pallas kernels, gather_columns(): pl.pallas_call(functools.partial(gather_kernel, ny, nz), out_shape=jax.Sh...  46.6 us
    all_to_all x1, waiting for transfers between devices, spread_weights(): lax.all_to_all(up_matrix.reshape(n, width, hidden), TENSOR, 0, 0, tiled=T...  33.5 us
    all_to_all x2, waiting for transfers between devices, spread_weights(): lax.all_to_all(down_blocks, TENSOR, 0, 0, tiled=True)  33.2 us
    unnamed x48, local copies, waits for them, and re-layouts  18.7 us
    all_to_all x2, starting transfers between devices, spread_weights(): lax.all_to_all(down_blocks, TENSOR, 0, 0, tiled=True)  11 us
  transfers between devices with their start and end apart: 5, of which 2 were waited for; matrix products, arithmetic and copies ran while one was open for 11% of the time, Pallas kernels for 31%

profile of v3, /device:TPU:38, one launch (start us, length us, event | category | flops | bytes accessed | tf_op | source)
XLA Modules:
  0.0 518.1 jit_solution(10431153617837081942)
XLA Ops:
  0.6 63.7 %all_to_all.20 = bf16[8,1024,128]{2,1,0:T(8,128)(2,1)} all-to-all(bf16[8,1024,128]{2,1,0:T(8,128)(2,1)} %bitcast.221), channel_id=1, replica_groups=mesh['section'=32,'ty'=4,'tz'=2] {'ty','tz'}, dimensions={0} | all-to-all | bytes 4194304 | tf_op jit(solution)/shard_map/all_to_all | solution.py:329
  64.3 3.6 all-to-all-start
  68.0 4.1 copy.25
  72.1 3.9 copy.26
  76.0 33.5 %all-to-all-done = bf16[8,1024,128]{2,1,0:T(8,128)(2,1)S(1)} async-done(((bf16[8,1024,128]{2,1,0:T(8,128)(2,1)}), bf16[8,1024,128]{2,1,0:T(8,128)(2,1)S(1)}, u32[]{:S(2)}, u32[]{:S(2)}) %all-to-all-start) | async-done | bytes 2097184 | tf_op jit(solution)/shard_map/all_to_all | solution.py:329
  109.6 1.4 copy-done.4
  110.9 6.7 %all-to-all-start.2 = ((bf16[8,128,1024]{2,1,0:T(8,128)(2,1)}), bf16[8,128,1024]{2,1,0:T(8,128)(2,1)S(1)}, u32[]{:S(2)}, u32[]{:S(2)}) async-start(bf16[8,128,1024]{2,1,0:T(8,128)(2,1)} %bitcast.218), calls=%async_computation.2 | async-start | bytes 4194304 | tf_op jit(solution)/shard_map/all_to_all | solution.py:332
  117.6 4.1 copy.27
  121.7 3.9 copy.28
  125.6 33.2 %all-to-all-done.2 = bf16[8,128,1024]{2,1,0:T(8,128)(2,1)S(1)} async-done(((bf16[8,128,1024]{2,1,0:T(8,128)(2,1)}), bf16[8,128,1024]{2,1,0:T(8,128)(2,1)S(1)}, u32[]{:S(2)}, u32[]{:S(2)}) %all-to-all-start.2) | async-done | bytes 2097184 | tf_op jit(solution)/shard_map/all_to_all | solution.py:332
  158.8 1.4 copy-done.2
  160.2 4.3 all-to-all-start.3
  164.8 1.4 fusion.27
  166.8 53.1 %shard_map.176 = f32[6,128]{1,0:T(8,128)} custom-call(f32[6,128]{1,0:T(8,128)} %reshape.275.v_ref), custom_call_target="tpu_custom_call" | custom-call | flops 6144 | bytes 49152 | tf_op jit(solution)/shard_map/pallas_call | solution.py:309
  226.7 2.9 copy.24
  229.6 4.0 copy.23
  233.6 2.5 convolution_bitcast_fusion.3
  238.5 1.9 pad_maximum_fusion.part_ref
  240.4 52.4 %shard_map.177 = f32[3,256,128]{2,1,0:T(8,128)} custom-call(f32[3,256,1024]{2,1,0:T(8,128)} %pad_maximum_fusion.part_ref), custom_call_target="tpu_custom_call" | custom-call | flops 786432 | bytes 3145728 | tf_op jit(solution)/shard_map/pallas_call | solution.py:241
  292.8 1.1 multiply_convert_fusion.4
  294.0 22.9 %shard_map.178 = bf16[2,256,1024]{2,1,0:T(8,128)(2,1)S(1)} custom-call(bf16[2,256,128]{2,1,0:T(8,128)(2,1)S(1)} %pad_maximum_fusion.2.x_ref), custom_call_target="tpu_custom_call" | custom-call | bytes 917504 | tf_op jit(solution)/shard_map/pallas_call | solution.py:135
  318.6 3.1 convert_reduce_fusion.3
  322.0 2.0 dynamic-slice_multiply_fusion
  326.4 11.2 %shard_map.180 = f32[1,128]{1,0:T(1,128)} custom-call(f32[1,128]{1,0:T(1,128)} %pad_bitcast_fusion.1.v_ref), custom_call_target="tpu_custom_call" | custom-call | flops 1024 | bytes 8192 | tf_op jit(solution)/shard_map/pallas_call | solution.py:309
  337.6 1.2 slice.95
  352.7 1.9 collective-permute-start
  354.9 2.0 multiply_reduce_fusion
  356.8 1.1 pad_bitcast_fusion.v_ref
  357.9 1.1 copy.34
  359.1 2.9 convert_reduce_fusion.2
  363.9 11.3 %shard_map.182 = f32[2,128]{1,0:T(2,128)} custom-call(f32[2,128]{1,0:T(2,128)} %bitcast.246), custom_call_target="tpu_custom_call" | custom-call | flops 2048 | bytes 16384 | tf_op jit(solution)/shard_map/pallas_call | solution.py:309
  375.2 2.6 fusion.23
  377.8 11.2 %shard_map.181 = f32[1,128]{1,0:T(1,128)} custom-call(f32[1,128]{1,0:T(1,128)} %pad_bitcast_fusion.v_ref), custom_call_target="tpu_custom_call" | custom-call | flops 1024 | bytes 8192 | tf_op jit(solution)/shard_map/pallas_call | solution.py:309
  389.0 2.2 collective-permute-start.1
  391.2 2.1 subtract_multiply_fusion
  393.3 3.3 convolution_bitcast_fusion.1
  396.6 1.9 fusion.32
  398.5 11.3 %shard_map.179 = f32[2,128]{1,0:T(2,128)} custom-call(f32[2,128]{1,0:T(2,128)} %bitcast.244), custom_call_target="tpu_custom_call" | custom-call | flops 2048 | bytes 16384 | tf_op jit(solution)/shard_map/pallas_call | solution.py:309
  411.2 2.6 convolution_bitcast_fusion
  413.9 2.0 pad_maximum_fusion.1.part_ref
  415.9 56.9 %shard_map.183 = f32[3,256,128]{2,1,0:T(8,128)} custom-call(f32[3,256,1024]{2,1,0:T(8,128)} %pad_maximum_fusion.1.part_ref), custom_call_target="tpu_custom_call" | custom-call | flops 786432 | bytes 3145728 | tf_op jit(solution)/shard_map/pallas_call | solution.py:241
  472.8 1.1 multiply_convert_fusion.2
  474.0 23.7 %shard_map.184 = bf16[2,256,1024]{2,1,0:T(8,128)(2,1)S(1)} custom-call(bf16[2,256,128]{2,1,0:T(8,128)(2,1)S(1)} %pad_maximum_fusion.3.x_ref), custom_call_target="tpu_custom_call" | custom-call | bytes 917504 | tf_op jit(solution)/shard_map/pallas_call | solution.py:135
  498.7 1.2 convert_reduce_fusion
  501.8 11.3 %shard_map.185 = f32[2,128]{1,0:T(2,128)} custom-call(f32[2,128]{1,0:T(2,128)} %bitcast.247), custom_call_target="tpu_custom_call" | custom-call | flops 2048 | bytes 16384 | tf_op jit(solution)/shard_map/pallas_call | solution.py:309
  513.1 1.1 copy.35
  514.3 1.2 convert_reduce_fusion.1
  515.5 2.5 fusion.45
  (71 shorter events, 18.9 us)
Async XLA Ops:
  0.6 223.2 %copy-start = (f32[1,8192]{1,0:T(1,128)S(1)}, f32[1,8192]{1,0:T(1,128)}, u32[]{:S(2)}) copy-start(f32[1,8192]{1,0:T(1,128)} %param.25) | copy-start | bytes 98308
  64.3 45.2 %all-to-all-start = ((bf16[8,1024,128]{2,1,0:T(8,128)(2,1)}), bf16[8,1024,128]{2,1,0:T(8,128)(2,1)S(1)}, u32[]{:S(2)}, u32[]{:S(2)}) async-start(bf16[8,1024,128]{2,1,0:T(8,128)(2,1)} %bitcast.222), calls=%async_computation | async-start | bytes 4194304 | tf_op jit(solution)/shard_map/all_to_all | solution.py:329
  109.6 1.4 copy-start.4
  110.9 47.9 %all-to-all-start.2 = ((bf16[8,128,1024]{2,1,0:T(8,128)(2,1)}), bf16[8,128,1024]{2,1,0:T(8,128)(2,1)S(1)}, u32[]{:S(2)}, u32[]{:S(2)}) async-start(bf16[8,128,1024]{2,1,0:T(8,128)(2,1)} %bitcast.218), calls=%async_computation.2 | async-start | bytes 4194304 | tf_op jit(solution)/shard_map/all_to_all | solution.py:332
  158.8 1.4 copy-start.2
  158.8 5.7 %copy-start.7 = (bf16[1,256,1024]{2,1,0:T(8,128)(2,1)S(1)}, bf16[1,256,1024]{2,1,0:T(8,128)(2,1)}, u32[]{:S(2)}) copy-start(bf16[1,256,1024]{2,1,0:T(8,128)(2,1)} %param.19) | copy-start | bytes 1572868
  158.8 5.9 %copy-start.6 = (bf16[1,256,1024]{2,1,0:T(8,128)(2,1)S(1)}, bf16[1,256,1024]{2,1,0:T(8,128)(2,1)}, u32[]{:S(2)}) copy-start(bf16[1,256,1024]{2,1,0:T(8,128)(2,1)} %param.17) | copy-start | bytes 1572868
  160.2 158.4 %all-to-all-start.3 = ((bf16[8,128,1024]{2,1,0:T(8,128)(2,1)}), bf16[8,128,1024]{2,1,0:T(8,128)(2,1)}, u32[]{:S(2)}, u32[]{:S(2)}) async-start(bf16[8,128,1024]{2,1,0:T(8,128)(2,1)} %bitcast.217), calls=%async_computation.3 | async-start | bytes 4194304 | tf_op jit(solution)/shard_map/all_to_all | solution.py:332
  164.6 56.0 %copy-start.19 = (s32[1,4]{1,0:T(1,128)S(1)}, s32[1,4]{1,0:T(1,128)}, u32[]{:S(2)}) copy-start(s32[1,4]{1,0:T(1,128)} %param.33) | copy-start | bytes 52
  164.6 60.0 %copy-start.17 = (s32[1,256]{1,0:T(1,128)S(1)}, s32[1,256]{1,0:T(1,128)}, u32[]{:S(2)}) copy-start(s32[1,256]{1,0:T(1,128)} %param.32) | copy-start | bytes 3076
  233.6 2.6 copy-start.8
  236.1 1.6 copy-start.1
  318.6 5.4 %copy-start.15 = (f32[1024,4]{0,1:T(4,128)S(1)}, f32[1024,4]{0,1:T(4,128)}, u32[]{:S(2)}) copy-start(f32[1024,4]{0,1:T(4,128)} %param.29) | copy-start | bytes 49156
  321.7 17.7 %copy-start.18 = (f32[4]{0:T(128)S(1)}, f32[4]{0:T(128)}, u32[]{:S(2)}) copy-start(f32[4]{0:T(128)} %param.30) | copy-start | bytes 52
  352.7 43.9 %collective-permute-start = (bf16[256,1024]{1,0:T(8,128)(2,1)}, bf16[256,1024]{1,0:T(8,128)(2,1)}, u32[]{:S(2)}, u32[]{:S(2)}) collective-permute-start(bf16[256,1024]{1,0:T(8,128)(2,1)} %fusion.31), channel_id=1, source_target_pairs={{0,8},{8,16},{16,24},{24,32},{32,40},{40,48},{48,56},{56,64},{64,7... | collective-permute-start | bytes 1572872 | tf_op jit(solution)/shard_map/ppermute | solution.py:20
  359.0 3.9 copy-start.9
  362.0 1.0 copy-start.13
  389.0 7.6 %copy-start.14 = (bf16[256,1024]{1,0:T(8,128)(2,1)S(1)}, bf16[256,1024]{1,0:T(8,128)(2,1)}, u32[]{:S(2)}) copy-start(bf16[256,1024]{1,0:T(8,128)(2,1)} %param.21) | copy-start | bytes 1572868
  389.0 22.3 %collective-permute-start.1 = (bf16[256,1024]{1,0:T(8,128)(2,1)}, bf16[256,1024]{1,0:T(8,128)(2,1)}, u32[]{:S(2)}, u32[]{:S(2)}) collective-permute-start(bf16[256,1024]{1,0:T(8,128)(2,1)} %fusion.23), channel_id=1, source_target_pairs={{8,0},{16,8},{24,16},{32,24},{40,32},{48,40},{56,48},{64,56},{72,6... | collective-permute-start | bytes 1572872 | tf_op jit(solution)/shard_map/ppermute | solution.py:20
  411.2 2.6 copy-start.12
  474.0 24.7 %copy-start.5 = (bf16[8,1024,128]{2,1,0:T(8,128)(2,1)S(1)}, bf16[8,1024,128]{2,1,0:T(8,128)(2,1)}, u32[]{:S(2)}) copy-start(bf16[8,1024,128]{2,1,0:T(8,128)(2,1)} %copy-done.4) | copy-start | bytes 6291460
  499.9 1.0 copy-start.10
  500.9 13.4 %copy-start.3 = (bf16[8,128,1024]{2,1,0:T(8,128)(2,1)S(1)}, bf16[8,128,1024]{2,1,0:T(8,128)(2,1)}, u32[]{:S(2)}) copy-start(bf16[8,128,1024]{2,1,0:T(8,128)(2,1)} %copy-done.2) | copy-start | bytes 6291460
  514.2 1.3 copy-start.11
  514.2 1.3 copy-start.16

commit v4 on v3

--- a/solution.py
+++ b/solution.py
@@ -378,8 +378,11 @@
     return (act_grad * sigmoid_pre * (1.0 + pre_act * (1.0 - sigmoid_pre))).astype(jnp.bfloat16)
 
 
-def back_finish(cotangent, norm_grad, scaled, inverse, gain_cols, full_width, collective):
-    row_total = row_sums(jnp.sum(scaled * gain_cols * norm_grad, axis=1), collective)
+def back_projection(scaled, gain_cols, norm_grad):
+    return jnp.sum(scaled * gain_cols * norm_grad, axis=1)
+
+
+def back_finish(cotangent, norm_grad, scaled, inverse, gain_cols, full_width, row_total):
     result = cotangent.astype(jnp.float32) + inverse * (
         gain_cols * norm_grad - scaled * row_total[:, None] / full_width
     )
@@ -428,9 +431,7 @@
     )
 
 
-def head_cotangent(
-    final_rows, head_gain, head_weight, head_bias, prompt_length, keep_mask, target_box
-):
+def head_pool(final_rows, head_gain, head_weight, prompt_length, keep_mask):
     row_count = keep_mask.shape[0]
     positions = jnp.arange(keep_mask.shape[1], dtype=jnp.int32)[None, :]
     starts = prompt_length[:, None]
@@ -439,7 +440,6 @@
     ) * keep_mask.astype(jnp.float32)
     counts = jnp.sum(weights, axis=1)
     local_width = final_rows.shape[1]
-    full_width = local_width * tensor_size()
     tokens = final_rows.astype(jnp.float32).reshape(row_count, keep_mask.shape[1], local_width)
     pooled = (
         jnp.einsum("rt,rtd->rd", weights, tokens, precision=lax.Precision.HIGHEST) / counts[:, None]
@@ -447,7 +447,12 @@
     gain_cols = lax.dynamic_slice_in_dim(head_gain, column_start(local_width), local_width, 0)
     logit_part = jnp.dot(pooled * gain_cols, head_weight, precision=lax.Precision.HIGHEST)
     square_part = jnp.sum(pooled * pooled, axis=1, keepdims=True)
-    totals = row_sums(jnp.concatenate([logit_part, square_part], axis=1), 5)
+    return (weights, counts, pooled, gain_cols), jnp.concatenate([logit_part, square_part], axis=1)
+
+
+def head_middle(pooled_state, totals, head_weight, head_bias, target_box):
+    weights, counts, pooled, gain_cols = pooled_state
+    full_width = pooled.shape[1] * tensor_size()
     inverse = lax.rsqrt(totals[:, 4] / full_width + epsilon)
     logits = totals[:, :4] * inverse[:, None] + head_bias
 
@@ -458,12 +463,18 @@
     logit_grad = pullback(jnp.ones((), jnp.float32))[0]
     scaled_grad = jnp.dot(logit_grad, head_weight.T, precision=lax.Precision.HIGHEST)
     unit_pooled = pooled * inverse[:, None]
-    row_total = row_sums(jnp.sum(unit_pooled * gain_cols * scaled_grad, axis=1), 6)
+    return (inverse, scaled_grad, unit_pooled), jnp.sum(unit_pooled * gain_cols * scaled_grad, axis=1)
+
+
+def head_finish(pooled_state, middle_state, row_total, row_shape):
+    weights, counts, pooled, gain_cols = pooled_state
+    inverse, scaled_grad, unit_pooled = middle_state
+    full_width = pooled.shape[1] * tensor_size()
     pooled_grad = inverse[:, None] * (
         gain_cols * scaled_grad - unit_pooled * row_total[:, None] / full_width
     )
     token_grad = (weights / counts[:, None])[:, :, None] * pooled_grad[:, None, :]
-    return token_grad.reshape(final_rows.shape[0], local_width).astype(jnp.bfloat16)
+    return token_grad.reshape(row_shape).astype(jnp.bfloat16)
 
 
 def per_device(
@@ -493,8 +504,6 @@
     full_width = width * tensor_size()
     last_gain_cols = lax.dynamic_slice_in_dim(last_gain[0], column_start(width), width, 0)
     first_gain_cols = lax.dynamic_slice_in_dim(first_gain[0], column_start(width), width, 0)
-    last_up_local, last_down_local = spread_weights(last_up[0], last_down[0])
-    first_up_local, first_down_local = spread_weights(first_up[0], first_down[0])
     closing_saved = jnp.where(closing, local_input, saved_last[0])
     squares = row_sums(
         jnp.stack(
@@ -502,6 +511,8 @@
         ),
         9,
     )
+    last_up_local, last_down_local = spread_weights(last_up[0], last_down[0])
+    first_up_local, first_down_local = spread_weights(first_up[0], first_down[0])
     last_pre = layer_forward(local_input, squares[0], last_gain_cols, last_up_local, full_width)
     first_pre, first_grad_part, first_scaled, first_inverse = layer_back_partials(
         saved_first[0], squares[1], first_cotangent[0], first_gain_cols, first_up_local,
@@ -514,18 +525,26 @@
     last_out = grouped_sum(spread[0], last_down_local, "rows")
     hidden_local = (local_input.astype(jnp.float32) + last_out).astype(jnp.bfloat16)
     first_norm_grad = grouped_sum(spread[1], first_up_local, "cols")
+    rows = first_norm_grad.shape[0]
+    pooled_state, head_part = head_pool(
+        hidden_local, head_gain, head_weight, prompt_length, keep_mask
+    )
+    first_projection = back_projection(first_scaled, first_gain_cols, first_norm_grad)
+    joined = row_sums(jnp.concatenate([first_projection, head_part.reshape(-1)]), 7)
     first_grad = back_finish(
         first_cotangent[0], first_norm_grad, first_scaled, first_inverse, first_gain_cols,
-        full_width, 7,
+        full_width, joined[:rows],
     )
     arrived_local = shifted(hidden_local, "section", 1)
     returned = shifted(first_grad, "section", -1)
-    head_grad = head_cotangent(
-        hidden_local, head_gain, head_weight, head_bias, prompt_length, keep_mask, target_box
+    middle_state, head_row = head_middle(
+        pooled_state, joined[rows:].reshape(head_part.shape), head_weight, head_bias, target_box
     )
     entry_local = jnp.where(opening, section_entry, arrived_local)
+    late_joined = row_sums(jnp.concatenate([local_squares(entry_local), head_row]), 10)
+    entry_squares = late_joined[:rows]
+    head_grad = head_finish(pooled_state, middle_state, late_joined[rows:], hidden_local.shape)
     cotangent = jnp.where(closing, head_grad, returned)
-    entry_squares = row_sums(local_squares(entry_local), 10)
     first_pre_late = layer_forward(entry_local, entry_squares, first_gain_cols, first_up_local, full_width)
     last_pre_late, last_grad_part, last_scaled, last_inverse = layer_back_partials(
         closing_saved, squares[2], cotangent, last_gain_cols, last_up_local, last_down_local,
@@ -540,8 +559,9 @@
     first_out = grouped_sum(spread_late[0], first_down_local, "rows")
     layer_output = (entry_local.astype(jnp.float32) + first_out).astype(jnp.bfloat16)
     last_norm_grad = grouped_sum(spread_late[1], last_up_local, "cols")
+    last_total = row_sums(back_projection(last_scaled, last_gain_cols, last_norm_grad), 8)
     input_gradient = back_finish(
-        cotangent, last_norm_grad, last_scaled, last_inverse, last_gain_cols, full_width, 8
+        cotangent, last_norm_grad, last_scaled, last_inverse, last_gain_cols, full_width, last_total
     )
     return (layer_output[None], input_gradient[None])
 

time: 520 us -> 491 us (0.944)
  Pallas kernels: 265 us -> 238 us
    pallas_call x6 -> x4, Pallas kernels: 109 us -> 87.1 us  [row_sums(): pl.pallas_call(functools.partial(sum_kernel, ny, nz), out_shape=jax.Shape...]
    pallas_call x2, Pallas kernels: 109 us -> 104 us  [reduce_columns(): pl.pallas_call(functools.partial(scatter_kernel, ny, nz), out_shape=jax.S...]
    unnamed x48 -> x64, local copies, waits for them, and re-layouts: 18.7 us -> 18.8 us
  transfers between devices with their start and end apart: 5 -> 5, of which waited for: 2 -> 3; matrix products, arithmetic and copies ran while one was open for 11% -> 10% of each run, Pallas kernels for 31% -> 29%
where the time goes in v4:
time: 491 us; the launch traced here: 489 us
  Pallas kernels  238 us (48%)
  waiting for transfers between devices  68.2 us (14%)
  blocking collectives  63.7 us (13%)
  local copies, waits for them, and re-layouts  38.6 us (8%)
  other arithmetic  25.6 us (5%)
  starting transfers between devices  20.5 us (4%)
  between operations  17.2 us (4%)
  matrix products  16.7 us (3%)
    pallas_call x2, Pallas kernels, reduce_columns(): pl.pallas_call(functools.partial(scatter_kernel, ny, nz), out_shape=jax.S...  104 us
    pallas_call x4, Pallas kernels, row_sums(): pl.pallas_call(functools.partial(sum_kernel, ny, nz), out_shape=jax.Shape...  87.1 us
    all_to_all x1, blocking collectives, spread_weights(): lax.all_to_all(up_matrix.reshape(n, width, hidden), TENSOR, 0, 0, tiled=T...  63.7 us
    pallas_call x2, Pallas kernels, gather_columns(): pl.pallas_call(functools.partial(gather_kernel, ny, nz), out_shape=jax.Sh...  47.3 us
    all_to_all x1, waiting for transfers between devices, spread_weights(): lax.all_to_all(up_matrix.reshape(n, width, hidden), TENSOR, 0, 0, tiled=T...  33.6 us
    all_to_all x2, waiting for transfers between devices, spread_weights(): lax.all_to_all(down_blocks, TENSOR, 0, 0, tiled=True)  33.3 us
    unnamed x64, local copies, waits for them, and re-layouts  18.8 us
    all_to_all x2, starting transfers between devices, spread_weights(): lax.all_to_all(down_blocks, TENSOR, 0, 0, tiled=True)  11 us
  transfers between devices with their start and end apart: 5, of which 3 were waited for; matrix products, arithmetic and copies ran while one was open for 10% of the time, Pallas kernels for 29%

profile of v4, /device:TPU:38, one launch (start us, length us, event | category | flops | bytes accessed | tf_op | source)
XLA Modules:
  0.0 488.6 jit_solution(12304501251782774578)
XLA Ops:
  0.6 63.7 %all_to_all.20 = bf16[8,1024,128]{2,1,0:T(8,128)(2,1)} all-to-all(bf16[8,1024,128]{2,1,0:T(8,128)(2,1)} %bitcast.223), channel_id=1, replica_groups=mesh['section'=32,'ty'=4,'tz'=2] {'ty','tz'}, dimensions={0} | all-to-all | bytes 4194304 | tf_op jit(solution)/shard_map/all_to_all | solution.py:329
  64.3 3.6 all-to-all-start
  68.0 4.1 copy.25
  72.0 3.9 copy.26
  75.9 33.6 %all-to-all-done = bf16[8,1024,128]{2,1,0:T(8,128)(2,1)S(1)} async-done(((bf16[8,1024,128]{2,1,0:T(8,128)(2,1)}), bf16[8,1024,128]{2,1,0:T(8,128)(2,1)S(1)}, u32[]{:S(2)}, u32[]{:S(2)}) %all-to-all-start) | async-done | bytes 2097184 | tf_op jit(solution)/shard_map/all_to_all | solution.py:329
  109.6 1.3 copy-done.5
  110.9 6.7 %all-to-all-start.2 = ((bf16[8,128,1024]{2,1,0:T(8,128)(2,1)}), bf16[8,128,1024]{2,1,0:T(8,128)(2,1)S(1)}, u32[]{:S(2)}, u32[]{:S(2)}) async-start(bf16[8,128,1024]{2,1,0:T(8,128)(2,1)} %bitcast.220), calls=%async_computation.2 | async-start | bytes 4194304 | tf_op jit(solution)/shard_map/all_to_all | solution.py:332
  117.6 4.1 copy.27
  121.7 3.9 copy.28
  125.6 33.2 %all-to-all-done.2 = bf16[8,128,1024]{2,1,0:T(8,128)(2,1)S(1)} async-done(((bf16[8,128,1024]{2,1,0:T(8,128)(2,1)}), bf16[8,128,1024]{2,1,0:T(8,128)(2,1)S(1)}, u32[]{:S(2)}, u32[]{:S(2)}) %all-to-all-start.2) | async-done | bytes 2097184 | tf_op jit(solution)/shard_map/all_to_all | solution.py:332
  158.8 1.3 copy-done.3
  160.2 4.3 all-to-all-start.3
  164.8 1.4 fusion.27
  166.8 53.1 %shard_map.176 = f32[6,128]{1,0:T(8,128)} custom-call(f32[6,128]{1,0:T(8,128)} %reshape.268.v_ref), custom_call_target="tpu_custom_call" | custom-call | flops 6144 | bytes 49152 | tf_op jit(solution)/shard_map/pallas_call | solution.py:309
  226.6 2.9 copy.24
  229.4 3.9 copy.23
  233.4 2.5 convolution_bitcast_fusion.3
  238.3 1.9 pad_maximum_fusion.part_ref
  240.2 52.4 %shard_map.177 = f32[3,256,128]{2,1,0:T(8,128)} custom-call(f32[3,256,1024]{2,1,0:T(8,128)} %pad_maximum_fusion.part_ref), custom_call_target="tpu_custom_call" | custom-call | flops 786432 | bytes 3145728 | tf_op jit(solution)/shard_map/pallas_call | solution.py:241
  292.5 1.1 multiply_convert_fusion.4
  293.7 22.8 %shard_map.178 = bf16[2,256,1024]{2,1,0:T(8,128)(2,1)S(1)} custom-call(bf16[2,256,128]{2,1,0:T(8,128)(2,1)S(1)} %pad_maximum_fusion.2.x_ref), custom_call_target="tpu_custom_call" | custom-call | bytes 917504 | tf_op jit(solution)/shard_map/pallas_call | solution.py:135
  318.3 3.1 convert_reduce_fusion.3
  322.4 1.0 copy-done.7
  323.4 1.2 convert_reduce_fusion.2
  325.6 1.9 dynamic-slice_multiply_fusion
  329.0 11.4 %shard_map.179 = f32[3,128]{1,0:T(4,128)} custom-call(f32[3,128]{1,0:T(4,128)} %fusion.67.v_ref), custom_call_target="tpu_custom_call" | custom-call | flops 3072 | bytes 24576 | tf_op jit(solution)/shard_map/pallas_call | solution.py:309
  355.4 1.4 fusion.31
  356.8 2.1 collective-permute-start
  358.9 1.2 fusion.23
  360.1 3.8 collective-permute-start.1
  364.2 2.0 multiply_reduce_fusion
  366.2 1.3 collective-permute-done
  367.7 1.3 fusion.66.v_ref
  369.0 1.7 convolution_bitcast_fusion.1
  370.8 11.3 %shard_map.180 = f32[3,128]{1,0:T(4,128)} custom-call(f32[3,128]{1,0:T(4,128)} %fusion.66.v_ref), custom_call_target="tpu_custom_call" | custom-call | flops 3072 | bytes 24576 | tf_op jit(solution)/shard_map/pallas_call | solution.py:309
  382.7 1.2 slice.120
  383.9 2.0 subtract_multiply_fusion
  386.7 2.6 convolution_bitcast_fusion
  389.3 2.0 pad_maximum_fusion.1.part_ref
  391.3 51.4 %shard_map.181 = f32[3,256,128]{2,1,0:T(8,128)} custom-call(f32[3,256,1024]{2,1,0:T(8,128)} %pad_maximum_fusion.1.part_ref), custom_call_target="tpu_custom_call" | custom-call | flops 786432 | bytes 3145728 | tf_op jit(solution)/shard_map/pallas_call | solution.py:241
  442.7 1.1 multiply_convert_fusion.2
  443.9 24.4 %shard_map.182 = bf16[2,256,1024]{2,1,0:T(8,128)(2,1)S(1)} custom-call(bf16[2,256,128]{2,1,0:T(8,128)(2,1)S(1)} %pad_maximum_fusion.3.x_ref), custom_call_target="tpu_custom_call" | custom-call | bytes 917504 | tf_op jit(solution)/shard_map/pallas_call | solution.py:135
  469.3 1.2 convert_reduce_fusion
  470.6 1.0 copy-done.13
  472.4 11.3 %shard_map.183 = f32[2,128]{1,0:T(2,128)} custom-call(f32[2,128]{1,0:T(2,128)} %bitcast.248), custom_call_target="tpu_custom_call" | custom-call | flops 2048 | bytes 16384 | tf_op jit(solution)/shard_map/pallas_call | solution.py:309
  483.7 1.1 copy.35
  484.9 1.2 convert_reduce_fusion.1
  486.1 2.5 fusion.45
  (88 shorter events, 17.8 us)
Async XLA Ops:
  0.6 223.2 %copy-start = (f32[1,8192]{1,0:T(1,128)S(1)}, f32[1,8192]{1,0:T(1,128)}, u32[]{:S(2)}) copy-start(f32[1,8192]{1,0:T(1,128)} %param.25) | copy-start | bytes 98308
  64.3 45.2 %all-to-all-start = ((bf16[8,1024,128]{2,1,0:T(8,128)(2,1)}), bf16[8,1024,128]{2,1,0:T(8,128)(2,1)S(1)}, u32[]{:S(2)}, u32[]{:S(2)}) async-start(bf16[8,1024,128]{2,1,0:T(8,128)(2,1)} %bitcast.224), calls=%async_computation | async-start | bytes 4194304 | tf_op jit(solution)/shard_map/all_to_all | solution.py:329
  109.6 1.3 copy-start.5
  110.9 47.9 %all-to-all-start.2 = ((bf16[8,128,1024]{2,1,0:T(8,128)(2,1)}), bf16[8,128,1024]{2,1,0:T(8,128)(2,1)S(1)}, u32[]{:S(2)}, u32[]{:S(2)}) async-start(bf16[8,128,1024]{2,1,0:T(8,128)(2,1)} %bitcast.220), calls=%async_computation.2 | async-start | bytes 4194304 | tf_op jit(solution)/shard_map/all_to_all | solution.py:332
  158.8 1.3 copy-start.3
  158.8 5.7 %copy-start.9 = (bf16[1,256,1024]{2,1,0:T(8,128)(2,1)S(1)}, bf16[1,256,1024]{2,1,0:T(8,128)(2,1)}, u32[]{:S(2)}) copy-start(bf16[1,256,1024]{2,1,0:T(8,128)(2,1)} %param.19) | copy-start | bytes 1572868
  158.8 5.9 %copy-start.8 = (bf16[1,256,1024]{2,1,0:T(8,128)(2,1)S(1)}, bf16[1,256,1024]{2,1,0:T(8,128)(2,1)}, u32[]{:S(2)}) copy-start(bf16[1,256,1024]{2,1,0:T(8,128)(2,1)} %param.17) | copy-start | bytes 1572868
  160.2 158.1 %all-to-all-start.3 = ((bf16[8,128,1024]{2,1,0:T(8,128)(2,1)}), bf16[8,128,1024]{2,1,0:T(8,128)(2,1)}, u32[]{:S(2)}, u32[]{:S(2)}) async-start(bf16[8,128,1024]{2,1,0:T(8,128)(2,1)} %bitcast.219), calls=%async_computation.3 | async-start | bytes 4194304 | tf_op jit(solution)/shard_map/all_to_all | solution.py:332
  164.5 56.1 %copy-start.27 = (s32[1,4]{1,0:T(1,128)S(1)}, s32[1,4]{1,0:T(1,128)}, u32[]{:S(2)}) copy-start(s32[1,4]{1,0:T(1,128)} %param.33) | copy-start | bytes 52
  164.5 60.0 %copy-start.25 = (s32[1,256]{1,0:T(1,128)S(1)}, s32[1,256]{1,0:T(1,128)}, u32[]{:S(2)}) copy-start(s32[1,256]{1,0:T(1,128)} %param.32) | copy-start | bytes 3076
  233.4 2.6 copy-start.10
  235.9 1.6 copy-start.1
  318.3 3.5 copy-start.20
  321.4 1.0 copy-start.17
  321.4 2.0 copy-start.7
  322.4 2.2 copy-start.11
  323.4 4.2 copy-start.22
  323.4 19.2 %copy-start.26 = (f32[4]{0:T(128)S(1)}, f32[4]{0:T(128)}, u32[]{:S(2)}) copy-start(f32[4]{0:T(128)} %param.30) | copy-start | bytes 52
  324.6 1.0 copy-start.15
  340.4 16.4 %copy-start.23 = (f32[3,128]{1,0:T(4,128)S(1)}, f32[3,128]{1,0:T(4,128)}, u32[]{:S(2)}) copy-start(f32[3,128]{1,0:T(4,128)} %shard_map.179) | copy-start | bytes 4612
  340.4 18.5 %copy-start.12 = (bf16[1,256,1024]{2,1,0:T(8,128)(2,1)S(1)}, bf16[1,256,1024]{2,1,0:T(8,128)(2,1)}, u32[]{:S(2)}) copy-start(bf16[1,256,1024]{2,1,0:T(8,128)(2,1)} %param.19) | copy-start | bytes 1572868
  340.4 18.5 %copy-start.16 = (f32[256,1024]{1,0:T(8,128)S(1)}, f32[256,1024]{1,0:T(8,128)}, u32[]{:S(2)}) copy-start(f32[256,1024]{1,0:T(8,128)} %copy-done.15) | copy-start | bytes 3145732
  340.4 18.5 %copy-start.19 = (bf16[1,256,1024]{2,1,0:T(8,128)(2,1)S(1)}, bf16[1,256,1024]{2,1,0:T(8,128)(2,1)}, u32[]{:S(2)}) copy-start(bf16[1,256,1024]{2,1,0:T(8,128)(2,1)} %param.20) | copy-start | bytes 1572868
  355.4 12.1 %copy-start.21 = (bf16[256,1024]{1,0:T(8,128)(2,1)S(1)}, bf16[256,1024]{1,0:T(8,128)(2,1)}, u32[]{:S(2)}) copy-start(bf16[256,1024]{1,0:T(8,128)(2,1)} %param.21) | copy-start | bytes 1572868
  356.8 12.2 %copy-start.2 = (bf16[1024,8,128]{0,2,1:T(8,128)(2,1)S(1)}, bf16[1024,8,128]{0,2,1:T(8,128)(2,1)}, u32[]{:S(2)}) copy-start(bf16[1024,8,128]{0,2,1:T(8,128)(2,1)} %copy.23) | copy-start | bytes 6291460
  356.8 10.6 %collective-permute-start = (bf16[256,1024]{1,0:T(8,128)(2,1)S(1)}, bf16[256,1024]{1,0:T(8,128)(2,1)S(1)}, u32[]{:S(2)}, u32[]{:S(2)}) collective-permute-start(bf16[256,1024]{1,0:T(8,128)(2,1)S(1)} %fusion.31), channel_id=1, source_target_pairs={{0,8},{8,16},{16,24},{24,32},{32,40},{40,48},{48,56},{56,64},{64,7... | collective-permute-start | bytes 1572872 | tf_op jit(solution)/shard_map/ppermute | solution.py:20
  360.1 26.6 %collective-permute-start.1 = (bf16[256,1024]{1,0:T(8,128)(2,1)}, bf16[256,1024]{1,0:T(8,128)(2,1)}, u32[]{:S(2)}, u32[]{:S(2)}) collective-permute-start(bf16[256,1024]{1,0:T(8,128)(2,1)} %fusion.23), channel_id=1, source_target_pairs={{8,0},{16,8},{24,16},{32,24},{40,32},{48,40},{56,48},{64,56},{72,6... | collective-permute-start | bytes 1572872 | tf_op jit(solution)/shard_map/ppermute | solution.py:20
  386.7 2.6 copy-start.18
  443.9 25.4 %copy-start.6 = (bf16[8,1024,128]{2,1,0:T(8,128)(2,1)S(1)}, bf16[8,1024,128]{2,1,0:T(8,128)(2,1)}, u32[]{:S(2)}) copy-start(bf16[8,1024,128]{2,1,0:T(8,128)(2,1)} %copy-done.5) | copy-start | bytes 6291460
  470.5 1.0 copy-start.13
  471.5 13.3 %copy-start.4 = (bf16[8,128,1024]{2,1,0:T(8,128)(2,1)S(1)}, bf16[8,128,1024]{2,1,0:T(8,128)(2,1)}, u32[]{:S(2)}) copy-start(bf16[8,128,1024]{2,1,0:T(8,128)(2,1)} %copy-done.3) | copy-start | bytes 6291460
  484.8 1.3 copy-start.14
  484.8 1.3 copy-start.24

commit v5 on v4

--- a/solution.py
+++ b/solution.py
@@ -511,8 +511,11 @@
         ),
         9,
     )
-    last_up_local, last_down_local = spread_weights(last_up[0], last_down[0])
-    first_up_local, first_down_local = spread_weights(first_up[0], first_down[0])
+    squares, up_last, down_last, up_first, down_first = lax.optimization_barrier(
+        (squares, last_up[0], last_down[0], first_up[0], first_down[0])
+    )
+    last_up_local, last_down_local = spread_weights(up_last, down_last)
+    first_up_local, first_down_local = spread_weights(up_first, down_first)
     last_pre = layer_forward(local_input, squares[0], last_gain_cols, last_up_local, full_width)
     first_pre, first_grad_part, first_scaled, first_inverse = layer_back_partials(
         saved_first[0], squares[1], first_cotangent[0], first_gain_cols, first_up_local,

time: 491 us -> 462 us (0.941)
  Pallas kernels: 238 us -> 204 us
  waiting for transfers between devices: 68.2 us -> 75 us
    pallas_call x4, Pallas kernels: 87.1 us -> 47.2 us  [row_sums(): pl.pallas_call(functools.partial(sum_kernel, ny, nz), out_shape=jax.Shape...]
    pallas_call x2, Pallas kernels: 104 us -> 121 us  [reduce_columns(): pl.pallas_call(functools.partial(scatter_kernel, ny, nz), out_shape=jax.S...]
    pallas_call x2, Pallas kernels: 47.3 us -> 35.9 us  [gather_columns(): pl.pallas_call(functools.partial(gather_kernel, ny, nz), out_shape=jax.Sh...]
    reshape x0 -> x2, local copies, waits for them, and re-layouts: none -> 7.92 us  [spread_weights(): down_blocks = down_matrix.reshape(hidden, n, width).transpose(1, 0, 2)]
    another operation x2 -> x1, local copies, waits for them, and re-layouts: 7.81 us -> 0.68 us  [row_sums(): return summed.reshape(-1)[:flat.shape[0]].reshape(shape)]
    unnamed x64 -> x48, local copies, waits for them, and re-layouts: 18.8 us -> 14.7 us
  transfers between devices with their start and end apart: 5 -> 5, of which waited for: 3 -> 2; matrix products, arithmetic and copies ran while one was open for 10% -> 9% of each run, Pallas kernels for 29% -> 21%
where the time goes in v5:
time: 462 us; the launch traced here: 460 us
  Pallas kernels  204 us (44%)
  waiting for transfers between devices  75 us (16%)
  blocking collectives  60.4 us (13%)
  local copies, waits for them, and re-layouts  35.9 us (8%)
  other arithmetic  27.8 us (6%)
  starting transfers between devices  20.7 us (4%)
  matrix products  18.3 us (4%)
  between operations  17.3 us (4%)
    pallas_call x2, Pallas kernels, reduce_columns(): pl.pallas_call(functools.partial(scatter_kernel, ny, nz), out_shape=jax.S...  121 us
    all_to_all x1, blocking collectives, spread_weights(): lax.all_to_all(up_matrix.reshape(n, width, hidden), TENSOR, 0, 0, tiled=T...  60.4 us
    pallas_call x4, Pallas kernels, row_sums(): pl.pallas_call(functools.partial(sum_kernel, ny, nz), out_shape=jax.Shape...  47.2 us
    all_to_all x1, waiting for transfers between devices, spread_weights(): lax.all_to_all(up_matrix.reshape(n, width, hidden), TENSOR, 0, 0, tiled=T...  37.6 us
    all_to_all x2, waiting for transfers between devices, spread_weights(): lax.all_to_all(down_blocks, TENSOR, 0, 0, tiled=True)  37.4 us
    pallas_call x2, Pallas kernels, gather_columns(): pl.pallas_call(functools.partial(gather_kernel, ny, nz), out_shape=jax.Sh...  35.9 us
    unnamed x48, local copies, waits for them, and re-layouts  14.7 us
    all_to_all x2, starting transfers between devices, spread_weights(): lax.all_to_all(down_blocks, TENSOR, 0, 0, tiled=True)  11.2 us
  transfers between devices with their start and end apart: 5, of which 2 were waited for; matrix products, arithmetic and copies ran while one was open for 9% of the time, Pallas kernels for 21%

profile of v5, /device:TPU:38, one launch (start us, length us, event | category | flops | bytes accessed | tf_op | source)
XLA Modules:
  0.0 459.8 jit_solution(16379594259480159176)
XLA Ops:
  0.7 1.4 fusion.24
  2.0 1.7 fusion.27
  4.4 13.3 %shard_map.176 = f32[6,128]{1,0:T(8,128)} custom-call(f32[6,128]{1,0:T(8,128)} %reshape.274.v_ref), custom_call_target="tpu_custom_call" | custom-call | flops 6144 | bytes 49152 | tf_op jit(solution)/shard_map/pallas_call | solution.py:309
  18.4 2.4 copy.24
  20.8 4.2 copy.25
  25.1 60.4 %all_to_all.20 = bf16[8,1024,128]{2,1,0:T(8,128)(2,1)} all-to-all(bf16[8,1024,128]{2,1,0:T(8,128)(2,1)S(1)} %bitcast.224), channel_id=1, replica_groups=mesh['section'=32,'ty'=4,'tz'=2] {'ty','tz'}, dimensions={0} | all-to-all | bytes 4194304 | tf_op jit(solution)/shard_map/all_to_all | solution.py:329
  85.5 3.6 all-to-all-start.1
  89.1 4.0 copy.28
  93.1 37.6 %all-to-all-done.1 = bf16[8,1024,128]{2,1,0:T(8,128)(2,1)S(1)} async-done(((bf16[8,1024,128]{2,1,0:T(8,128)(2,1)}), bf16[8,1024,128]{2,1,0:T(8,128)(2,1)S(1)}, u32[]{:S(2)}, u32[]{:S(2)}) %all-to-all-start.1) | async-done | bytes 2097184 | tf_op jit(solution)/shard_map/all_to_all | solution.py:329
  130.7 1.3 copy-done.4
  132.0 6.7 %all-to-all-start.2 = ((bf16[8,128,1024]{2,1,0:T(8,128)(2,1)}), bf16[8,128,1024]{2,1,0:T(8,128)(2,1)}, u32[]{:S(2)}, u32[]{:S(2)}) async-start(bf16[8,128,1024]{2,1,0:T(8,128)(2,1)} %bitcast.222), calls=%async_computation.2 | async-start | bytes 4194304 | tf_op jit(solution)/shard_map/all_to_all | solution.py:332
  138.7 3.9 copy.30
  142.7 37.4 %all-to-all-done.2 = bf16[8,128,1024]{2,1,0:T(8,128)(2,1)} async-done(((bf16[8,128,1024]{2,1,0:T(8,128)(2,1)}), bf16[8,128,1024]{2,1,0:T(8,128)(2,1)}, u32[]{:S(2)}, u32[]{:S(2)}) %all-to-all-start.2) | async-done | bytes 2097184 | tf_op jit(solution)/shard_map/all_to_all | solution.py:332
  180.1 4.5 all-to-all-start.3
  190.6 2.9 copy.27
  193.5 4.0 copy.26
  197.5 2.4 convolution_bitcast_fusion.3
  202.3 2.1 pad_maximum_fusion.part_ref
  204.4 66.6 %shard_map.177 = f32[3,256,128]{2,1,0:T(8,128)} custom-call(f32[3,256,1024]{2,1,0:T(8,128)} %pad_maximum_fusion.part_ref), custom_call_target="tpu_custom_call" | custom-call | flops 786432 | bytes 3145728 | tf_op jit(solution)/shard_map/pallas_call | solution.py:241
  271.0 1.1 multiply_convert_fusion.4
  272.1 16.7 %shard_map.178 = bf16[2,256,1024]{2,1,0:T(8,128)(2,1)S(1)} custom-call(bf16[2,256,128]{2,1,0:T(8,128)(2,1)S(1)} %pad_maximum_fusion.2.x_ref), custom_call_target="tpu_custom_call" | custom-call | bytes 917504 | tf_op jit(solution)/shard_map/pallas_call | solution.py:135
  288.9 0.9 copy.36
  290.6 1.2 convert_reduce_fusion.2
  291.8 1.0 copy-done.10
  293.2 3.1 convert_reduce_fusion.3
  296.6 2.0 dynamic-slice_multiply_fusion
  300.1 1.0 fusion.31
  301.0 11.3 %shard_map.179 = f32[3,128]{1,0:T(4,128)} custom-call(f32[3,128]{1,0:T(4,128)} %fusion.67.v_ref), custom_call_target="tpu_custom_call" | custom-call | flops 3072 | bytes 24576 | tf_op jit(solution)/shard_map/pallas_call | solution.py:309
  327.9 2.1 collective-permute-start
  329.9 2.7 fusion.23
  332.6 3.8 collective-permute-start.1
  336.7 2.0 multiply_reduce_fusion
  339.0 1.2 fusion.66.v_ref
  340.2 1.8 convolution_bitcast_fusion.1
  342.0 11.3 %shard_map.180 = f32[3,128]{1,0:T(4,128)} custom-call(f32[3,128]{1,0:T(4,128)} %fusion.66.v_ref), custom_call_target="tpu_custom_call" | custom-call | flops 3072 | bytes 24576 | tf_op jit(solution)/shard_map/pallas_call | solution.py:309
  354.0 1.2 slice.117
  355.1 2.0 subtract_multiply_fusion
  358.0 2.6 convolution_bitcast_fusion
  360.6 2.0 pad_maximum_fusion.1.part_ref
  362.6 54.7 %shard_map.181 = f32[3,256,128]{2,1,0:T(8,128)} custom-call(f32[3,256,1024]{2,1,0:T(8,128)} %pad_maximum_fusion.1.part_ref), custom_call_target="tpu_custom_call" | custom-call | flops 786432 | bytes 3145728 | tf_op jit(solution)/shard_map/pallas_call | solution.py:241
  417.3 1.1 multiply_convert_fusion.2
  418.5 19.2 %shard_map.182 = bf16[2,256,1024]{2,1,0:T(8,128)(2,1)S(1)} custom-call(bf16[2,256,128]{2,1,0:T(8,128)(2,1)S(1)} %pad_maximum_fusion.3.x_ref), custom_call_target="tpu_custom_call" | custom-call | bytes 917504 | tf_op jit(solution)/shard_map/pallas_call | solution.py:135
  438.7 1.2 convert_reduce_fusion
  439.9 1.0 copy-done.8
  441.8 11.3 %shard_map.183 = f32[2,128]{1,0:T(2,128)} custom-call(f32[2,128]{1,0:T(2,128)} %bitcast.255), custom_call_target="tpu_custom_call" | custom-call | flops 2048 | bytes 16384 | tf_op jit(solution)/shard_map/pallas_call | solution.py:309
  453.1 1.1 copy.38
  454.3 3.0 convert_reduce_fusion.1
  457.2 2.5 fusion.45
  (73 shorter events, 15.9 us)
Async XLA Ops:
  0.6 187.9 %copy-start = (f32[1,8192]{1,0:T(1,128)S(1)}, f32[1,8192]{1,0:T(1,128)}, u32[]{:S(2)}) copy-start(f32[1,8192]{1,0:T(1,128)} %param.22) | copy-start | bytes 98308
  0.6 17.7 %copy-start.12 = (bf16[1,128,8192]{2,1,0:T(8,128)(2,1)S(1)}, bf16[1,128,8192]{2,1,0:T(8,128)(2,1)}, u32[]{:S(2)}) copy-start(bf16[1,128,8192]{2,1,0:T(8,128)(2,1)} %param.24) | copy-start | bytes 6291460
  20.8 4.2 copy-start.13
  85.5 45.2 %all-to-all-start.1 = ((bf16[8,1024,128]{2,1,0:T(8,128)(2,1)}), bf16[8,1024,128]{2,1,0:T(8,128)(2,1)S(1)}, u32[]{:S(2)}, u32[]{:S(2)}) async-start(bf16[8,1024,128]{2,1,0:T(8,128)(2,1)} %bitcast.225), calls=%async_computation.1 | async-start | bytes 4194304 | tf_op jit(solution)/shard_map/all_to_all | solution.py:329
  130.7 1.3 copy-start.4
  132.0 48.1 %all-to-all-start.2 = ((bf16[8,128,1024]{2,1,0:T(8,128)(2,1)}), bf16[8,128,1024]{2,1,0:T(8,128)(2,1)}, u32[]{:S(2)}, u32[]{:S(2)}) async-start(bf16[8,128,1024]{2,1,0:T(8,128)(2,1)} %bitcast.222), calls=%async_computation.2 | async-start | bytes 4194304 | tf_op jit(solution)/shard_map/all_to_all | solution.py:332
  180.1 5.1 %copy-start.19 = (s32[1,4]{1,0:T(1,128)S(1)}, s32[1,4]{1,0:T(1,128)}, u32[]{:S(2)}) copy-start(s32[1,4]{1,0:T(1,128)} %param.33) | copy-start | bytes 52
  180.1 9.1 %copy-start.17 = (s32[1,256]{1,0:T(1,128)S(1)}, s32[1,256]{1,0:T(1,128)}, u32[]{:S(2)}) copy-start(s32[1,256]{1,0:T(1,128)} %param.32) | copy-start | bytes 3076
  180.1 113.0 %all-to-all-start.3 = ((bf16[8,128,1024]{2,1,0:T(8,128)(2,1)}), bf16[8,128,1024]{2,1,0:T(8,128)(2,1)}, u32[]{:S(2)}, u32[]{:S(2)}) async-start(bf16[8,128,1024]{2,1,0:T(8,128)(2,1)} %bitcast.31), calls=%async_computation.3 | async-start | bytes 4194304 | tf_op jit(solution)/shard_map/all_to_all | solution.py:332
  193.5 4.0 copy-start.14
  197.5 2.4 copy-start.7
  199.9 1.6 copy-start.1
  199.9 1.7 copy-start.6
  288.8 1.8 copy-start.5
  291.8 1.0 copy-start.10
  293.1 5.4 %copy-start.15 = (f32[1024,4]{0,1:T(4,128)S(1)}, f32[1024,4]{0,1:T(4,128)}, u32[]{:S(2)}) copy-start(f32[1024,4]{0,1:T(4,128)} %param.29) | copy-start | bytes 49156
  296.2 18.7 %copy-start.18 = (f32[4]{0:T(128)S(1)}, f32[4]{0:T(128)}, u32[]{:S(2)}) copy-start(f32[4]{0:T(128)} %param.30) | copy-start | bytes 52
  327.9 12.4 %copy-start.2 = (bf16[1024,8,128]{0,2,1:T(8,128)(2,1)S(1)}, bf16[1024,8,128]{0,2,1:T(8,128)(2,1)}, u32[]{:S(2)}) copy-start(bf16[1024,8,128]{0,2,1:T(8,128)(2,1)} %copy.26) | copy-start | bytes 6291460
  327.9 10.9 %collective-permute-start = (bf16[256,1024]{1,0:T(8,128)(2,1)}, bf16[256,1024]{1,0:T(8,128)(2,1)S(1)}, u32[]{:S(2)}, u32[]{:S(2)}) collective-permute-start(bf16[256,1024]{1,0:T(8,128)(2,1)} %fusion.31), channel_id=1, source_target_pairs={{0,8},{8,16},{16,24},{24,32},{32,40},{40,48},{48,56},{56,64},{64,7... | collective-permute-start | bytes 1572872 | tf_op jit(solution)/shard_map/ppermute | solution.py:20
  332.6 25.3 %collective-permute-start.1 = (bf16[256,1024]{1,0:T(8,128)(2,1)}, bf16[256,1024]{1,0:T(8,128)(2,1)}, u32[]{:S(2)}, u32[]{:S(2)}) collective-permute-start(bf16[256,1024]{1,0:T(8,128)(2,1)} %fusion.23), channel_id=1, source_target_pairs={{8,0},{16,8},{24,16},{32,24},{40,32},{48,40},{56,48},{64,56},{72,6... | collective-permute-start | bytes 1572872 | tf_op jit(solution)/shard_map/ppermute | solution.py:20
  357.9 2.6 copy-start.11
  418.4 20.2 %copy-start.3 = (bf16[8,1024,128]{2,1,0:T(8,128)(2,1)S(1)}, bf16[8,1024,128]{2,1,0:T(8,128)(2,1)}, u32[]{:S(2)}) copy-start(bf16[8,1024,128]{2,1,0:T(8,128)(2,1)} %all_to_all.20) | copy-start | bytes 6291460
  439.9 1.0 copy-start.8
  454.2 3.0 copy-start.9
  454.2 3.0 copy-start.16

commit v6 on v5

--- a/solution.py
+++ b/solution.py
@@ -322,15 +322,90 @@
     return summed.reshape(-1)[: flat.shape[0]].reshape(shape)
 
 
-def spread_weights(up_matrix, down_matrix):
-    n = tensor_size()
-    full, hidden = up_matrix.shape
-    width = full // n
-    up_blocks = lax.all_to_all(up_matrix.reshape(n, width, hidden), TENSOR, 0, 0, tiled=True)
-    up_local = up_blocks.transpose(1, 0, 2).reshape(width, n * hidden)
-    down_blocks = down_matrix.reshape(hidden, n, width).transpose(1, 0, 2)
-    down_local = lax.all_to_all(down_blocks, TENSOR, 0, 0, tiled=True).reshape(n * hidden, width)
-    return up_local, down_local
+def spread_kernel(ny, nz, *refs):
+    ups_in, downs_in = refs[0:4:2], refs[1:4:2]
+    ups_out, downs_out = refs[4:8:2], refs[5:8:2]
+    send_sems, recv_sems, local_sems = refs[8:]
+    n = ny * nz
+    ty, tz = lax.axis_index("ty"), lax.axis_index("tz")
+    me = ty * nz + tz
+    section = lax.axis_index("section")
+    width, hidden = ups_in[0].shape[0] // n, ups_in[0].shape[1]
+    peers = [(lax.rem(ty + dy, ny), lax.rem(tz + dz, nz)) for dy in range(ny) for dz in range(nz)][1:]
+
+    def up_rows(index):
+        return pl.ds(pl.multiple_of(index * width, width), width)
+
+    def hidden_part(index):
+        return pl.ds(pl.multiple_of(index * hidden, hidden), hidden)
+
+    pieces = []
+    for layer in range(2):
+        up_in, down_in, up_out, down_out = ups_in[layer], downs_in[layer], ups_out[layer], downs_out[layer]
+        pieces.append(
+            (lambda i, r=up_in: r.at[up_rows(i), :], lambda i, r=up_out: r.at[:, hidden_part(i)])
+        )
+        pieces.append(
+            (lambda i, r=down_in: r.at[:, up_rows(i)], lambda i, r=down_out: r.at[hidden_part(i), :])
+        )
+
+    barrier = pltpu.get_barrier_semaphore()
+    for y, z in peers:
+        pl.semaphore_signal(barrier, inc=1, device_id=(section, y, z), device_id_type=MESH_ID)
+    pl.semaphore_wait(barrier, len(peers))
+    started, own_copies = [], []
+    for piece, (source, target) in enumerate(pieces):
+        for number, (y, z) in enumerate(peers):
+            copy = pltpu.make_async_remote_copy(
+                src_ref=source(y * nz + z),
+                dst_ref=target(me),
+                send_sem=send_sems.at[piece, number],
+                recv_sem=recv_sems.at[piece, me],
+                device_id=(section, y, z),
+                device_id_type=MESH_ID,
+            )
+            copy.start()
+            started.append(copy)
+        own = pltpu.make_async_copy(source(me), target(me), local_sems.at[piece])
+        own.start()
+        own_copies.append(own)
+    for piece, (source, target) in enumerate(pieces):
+        for y, z in peers:
+            index = y * nz + z
+            pltpu.make_async_remote_copy(
+                src_ref=source(index),
+                dst_ref=target(index),
+                send_sem=send_sems.at[piece, 0],
+                recv_sem=recv_sems.at[piece, index],
+                device_id=(section, y, z),
+                device_id_type=MESH_ID,
+            ).wait_recv()
+    for copy in own_copies:
+        copy.wait()
+    for copy in started:
+        copy.wait_send()
+
+
+def spread_weights(last_up, last_down, first_up, first_down):
+    ny, nz = lax.axis_size("ty"), lax.axis_size("tz")
+    n = ny * nz
+    full, hidden = last_up.shape
+    up_shape = jax.ShapeDtypeStruct((full // n, n * hidden), last_up.dtype)
+    down_shape = jax.ShapeDtypeStruct((n * hidden, full // n), last_down.dtype)
+    moved = 4 * last_up.size * last_up.dtype.itemsize
+    return pl.pallas_call(
+        functools.partial(spread_kernel, ny, nz),
+        out_shape=(up_shape, down_shape, up_shape, down_shape),
+        in_specs=[pl.BlockSpec(memory_space=pl.ANY)] * 4,
+        out_specs=(pl.BlockSpec(memory_space=pl.ANY),) * 4,
+        scratch_shapes=[
+            pltpu.SemaphoreType.DMA((4, n - 1)),
+            pltpu.SemaphoreType.DMA((4, n)),
+            pltpu.SemaphoreType.DMA((4,)),
+        ],
+        compiler_params=pltpu.CompilerParams(collective_id=11, has_side_effects=True),
+        cost_estimate=pl.CostEstimate(flops=0, transcendentals=0, bytes_accessed=moved),
+    )(last_up, last_down, first_up, first_down)
 
 
 def grouped_sum(left, right, contract):
@@ -514,8 +589,9 @@
     squares, up_last, down_last, up_first, down_first = lax.optimization_barrier(
         (squares, last_up[0], last_down[0], first_up[0], first_down[0])
     )
-    last_up_local, last_down_local = spread_weights(up_last, down_last)
-    first_up_local, first_down_local = spread_weights(up_first, down_first)
+    last_up_local, last_down_local, first_up_local, first_down_local = spread_weights(
+        up_last, down_last, up_first, down_first
+    )
     last_pre = layer_forward(local_input, squares[0], last_gain_cols, last_up_local, full_width)
     first_pre, first_grad_part, first_scaled, first_inverse = layer_back_partials(
         saved_first[0], squares[1], first_cotangent[0], first_gain_cols, first_up_local,

time: 462 us -> 474 us (1.026)
  the two profiles are of different devices: /device:TPU:38 before, /device:TPU:4 now
where the time goes in v6:
time: 474 us; the launch traced here: 473 us
  Pallas kernels  394 us (83%)
  other arithmetic  29 us (6%)
  matrix products  18.3 us (4%)
  between operations  17.7 us (4%)
  local copies, waits for them, and re-layouts  9.15 us (2%)
    pallas_call x1, Pallas kernels, spread_weights(): pl.pallas_call(functools.partial(spread_kernel, ny, nz), out_shape=(up_sh...  190 us
    pallas_call x2, Pallas kernels, reduce_columns(): pl.pallas_call(functools.partial(scatter_kernel, ny, nz), out_shape=jax.S...  119 us
    pallas_call x4, Pallas kernels, row_sums(): pl.pallas_call(functools.partial(sum_kernel, ny, nz), out_shape=jax.Shape...  48.4 us
    pallas_call x2, Pallas kernels, gather_columns(): pl.pallas_call(functools.partial(gather_kernel, ny, nz), out_shape=jax.Sh...  36.5 us
  transfers between devices with their start and end apart: 2, of which 0 were waited for; matrix products, arithmetic and copies ran while one was open for 3% of the time, Pallas kernels for 2%

profile of v6, /device:TPU:4, one launch (start us, length us, event | category | flops | bytes accessed | tf_op | source)
XLA Modules:
  0.0 472.7 jit_solution(6342454001519751518)
XLA Ops:
  0.7 1.2 fusion.32
  1.9 1.7 fusion.33
  4.2 14.2 %shard_map.176 = f32[6,128]{1,0:T(8,128)} custom-call(f32[6,128]{1,0:T(8,128)} %reshape.220.v_ref), custom_call_target="tpu_custom_call" | custom-call | flops 6144 | bytes 49152 | tf_op jit(solution)/shard_map/pallas_call | solution.py:309
  18.5 0.7 reshape_reshape.3
  19.2 190.5 %shard_map.177 = (bf16[1024,1024]{1,0:T(8,128)(2,1)}, bf16[1024,1024]{1,0:T(8,128)(2,1)}, bf16[1024,1024]{1,0:T(8,128)(2,1)}, bf16[1024,1024]{1,0:T(8,128)(2,1)}) custom-call(bf16[8192,128]{1,0:T(8,128)(2,1)} %bitcast.177, bf16[128,8192]{1,0:T(8,128)(2,1)} %bitcast.178, bf16[8192,128]{1,0:T(8,128)(2,1)} %bitcast.179, bf16[128,8192]{1,0:T(8,128)(2,1)} %bitcast.180), custom_call_target="tpu_custom_call" | custom-call | bytes 8388608 | tf_op jit(solution)/shard_map/pallas_call | solution.py:396
  209.7 3.5 convolution_bitcast_fusion.3
  213.1 0.9 constant_dynamic-slice_fusion
  214.0 2.3 convolution_bitcast_fusion.4
  216.4 0.8 convolution_bitcast_fusion.5
  217.6 2.1 pad_maximum_fusion.part_ref
  219.7 58.5 %shard_map.178 = f32[3,256,128]{2,1,0:T(8,128)} custom-call(f32[3,256,1024]{2,1,0:T(8,128)} %pad_maximum_fusion.part_ref), custom_call_target="tpu_custom_call" | custom-call | flops 786432 | bytes 3145728 | tf_op jit(solution)/shard_map/pallas_call | solution.py:241
  278.2 1.1 multiply_convert_fusion.4
  279.4 19.4 %shard_map.179 = bf16[2,256,1024]{2,1,0:T(8,128)(2,1)S(1)} custom-call(bf16[2,256,128]{2,1,0:T(8,128)(2,1)S(1)} %pad_maximum_fusion.2.x_ref), custom_call_target="tpu_custom_call" | custom-call | bytes 917504 | tf_op jit(solution)/shard_map/pallas_call | solution.py:135
  299.0 1.3 convert_reduce_fusion.2
  302.3 1.2 convert_reduce_fusion.3
  303.5 0.8 fusion.86
  304.7 2.0 dynamic-slice_multiply_fusion
  306.9 0.8 maximum_bitcast_fusion
  308.2 11.3 %shard_map.180 = f32[3,128]{1,0:T(4,128)} custom-call(f32[3,128]{1,0:T(4,128)} %fusion.65.v_ref), custom_call_target="tpu_custom_call" | custom-call | flops 3072 | bytes 24576 | tf_op jit(solution)/shard_map/pallas_call | solution.py:309
  319.6 0.8 slice_bitcast_fusion.4
  320.4 2.6 fusion.26
  322.9 1.9 collective-permute-start.1
  325.0 2.6 collective-permute-start
  327.6 0.7 slice_bitcast_fusion.5
  329.6 0.7 fusion.89
  330.2 0.7 fusion.88
  346.0 2.0 multiply_reduce_fusion
  348.0 1.7 convolution_bitcast_fusion.1
  349.7 1.3 fusion.34
  351.0 1.2 fusion.64.v_ref
  352.2 0.7 broadcast_divide_fusion.1
  352.9 11.5 %shard_map.181 = f32[3,128]{1,0:T(4,128)} custom-call(f32[3,128]{1,0:T(4,128)} %fusion.64.v_ref), custom_call_target="tpu_custom_call" | custom-call | flops 3072 | bytes 24576 | tf_op jit(solution)/shard_map/pallas_call | solution.py:309
  364.4 0.8 rsqrt_bitcast_fusion
  365.2 1.2 slice.117
  366.4 2.0 subtract_multiply_fusion
  368.4 2.4 convolution_bitcast_fusion.2
  370.8 1.9 convolution_bitcast_fusion
  372.8 1.9 pad_maximum_fusion.1.part_ref
  374.7 60.3 %shard_map.182 = f32[3,256,128]{2,1,0:T(8,128)} custom-call(f32[3,256,1024]{2,1,0:T(8,128)} %pad_maximum_fusion.1.part_ref), custom_call_target="tpu_custom_call" | custom-call | flops 786432 | bytes 3145728 | tf_op jit(solution)/shard_map/pallas_call | solution.py:241
  434.9 1.1 multiply_convert_fusion.2
  436.1 17.1 %shard_map.183 = bf16[2,256,1024]{2,1,0:T(8,128)(2,1)S(1)} custom-call(bf16[2,256,128]{2,1,0:T(8,128)(2,1)S(1)} %pad_maximum_fusion.3.x_ref), custom_call_target="tpu_custom_call" | custom-call | bytes 917504 | tf_op jit(solution)/shard_map/pallas_call | solution.py:135
  453.4 1.2 convert_reduce_fusion.1
  454.6 1.0 fusion.39
  455.7 1.3 convert_reduce_fusion
  456.9 1.0 copy-done.9
  457.9 0.9 fusion.16
  458.8 11.3 %shard_map.184 = f32[2,128]{1,0:T(2,128)} custom-call(f32[2,128]{1,0:T(2,128)} %bitcast.211), custom_call_target="tpu_custom_call" | custom-call | flops 2048 | bytes 16384 | tf_op jit(solution)/shard_map/pallas_call | solution.py:309
  470.1 2.6 fusion.45
  (59 shorter events, 4.5 us)
Async XLA Ops:
  0.6 306.1 %copy-start = (f32[1024,4]{0,1:T(4,128)S(1)}, f32[1024,4]{0,1:T(4,128)}, u32[]{:S(2)}) copy-start(f32[1024,4]{0,1:T(4,128)} %param.29) | copy-start | bytes 49156
  19.2 190.5 %copy-start.12 = (bf16[1,256,1024]{2,1,0:T(8,128)(2,1)S(1)}, bf16[1,256,1024]{2,1,0:T(8,128)(2,1)}, u32[]{:S(2)}) copy-start(bf16[1,256,1024]{2,1,0:T(8,128)(2,1)} %param.20) | copy-start | bytes 1572868
  209.6 4.3 copy-start.3
  213.1 3.2 copy-start.1
  213.1 3.2 copy-start.4
  216.3 1.2 copy-start.11
  279.4 19.6 %copy-start.2 = (bf16[1024,1024]{1,0:T(8,128)(2,1)S(1)}, bf16[1024,1024]{1,0:T(8,128)(2,1)}, u32[]{:S(2)}) copy-start(bf16[1024,1024]{1,0:T(8,128)(2,1)} %get-tuple-element.17) | copy-start | bytes 6291460
  300.3 3.2 copy-start.6
  300.3 2.0 copy-start.16
  301.8 1.7 copy-start.13
  303.5 1.2 copy-start.7
  319.5 5.3 %copy-start.5 = (bf16[1,256,1024]{2,1,0:T(8,128)(2,1)S(1)}, bf16[1,256,1024]{2,1,0:T(8,128)(2,1)}, u32[]{:S(2)}) copy-start(bf16[1,256,1024]{2,1,0:T(8,128)(2,1)} %param.17) | copy-start | bytes 1572868
  319.6 5.3 %copy-start.8 = (f32[256,1024]{1,0:T(8,128)S(1)}, f32[256,1024]{1,0:T(8,128)}, u32[]{:S(2)}) copy-start(f32[256,1024]{1,0:T(8,128)} %copy-done.7) | copy-start | bytes 3145732
  320.3 9.2 %copy-start.14 = (f32[4]{0:T(128)S(1)}, f32[4]{0:T(128)}, u32[]{:S(2)}) copy-start(f32[4]{0:T(128)} %param.30) | copy-start | bytes 52
  320.4 9.9 %copy-start.18 = (s32[1,4]{1,0:T(1,128)S(1)}, s32[1,4]{1,0:T(1,128)}, u32[]{:S(2)}) copy-start(s32[1,4]{1,0:T(1,128)} %param.33) | copy-start | bytes 52
  322.9 47.9 %collective-permute-start.1 = (bf16[256,1024]{1,0:T(8,128)(2,1)}, bf16[256,1024]{1,0:T(8,128)(2,1)}, u32[]{:S(2)}, u32[]{:S(2)}) collective-permute-start(bf16[256,1024]{1,0:T(8,128)(2,1)} %fusion.26), channel_id=1, source_target_pairs={{8,0},{16,8},{24,16},{32,24},{40,32},{48,40},{56,48},{64,56},{72,6... | collective-permute-start | bytes 1572872 | tf_op jit(solution)/shard_map/ppermute | solution.py:20
  325.0 24.7 %collective-permute-start = (bf16[256,1024]{1,0:T(8,128)(2,1)S(1)}, bf16[256,1024]{1,0:T(8,128)(2,1)}, u32[]{:S(2)}, u32[]{:S(2)}) collective-permute-start(bf16[256,1024]{1,0:T(8,128)(2,1)S(1)} %fusion.30), channel_id=1, source_target_pairs={{0,8},{8,16},{16,24},{24,32},{32,40},{40,48},{48,56},{56,64},{64,7... | collective-permute-start | bytes 1572872 | tf_op jit(solution)/shard_map/ppermute | solution.py:20
  364.4 6.4 %copy-start.17 = (bf16[1024,1024]{1,0:T(8,128)(2,1)S(1)}, bf16[1024,1024]{1,0:T(8,128)(2,1)}, u32[]{:S(2)}) copy-start(bf16[1024,1024]{1,0:T(8,128)(2,1)} %get-tuple-element.19) | copy-start | bytes 6291460
  370.8 2.0 copy-start.10
  436.1 17.3 %copy-start.15 = (bf16[1024,1024]{1,0:T(8,128)(2,1)S(1)}, bf16[1024,1024]{1,0:T(8,128)(2,1)}, u32[]{:S(2)}) copy-start(bf16[1024,1024]{1,0:T(8,128)(2,1)} %get-tuple-element.18) | copy-start | bytes 6291460
  456.9 1.0 copy-start.9

commit v7 on v6

--- a/solution.py
+++ b/solution.py
@@ -369,6 +369,8 @@
         own = pltpu.make_async_copy(source(me), target(me), local_sems.at[piece])
         own.start()
         own_copies.append(own)
+        for copy in started[-len(peers):]:
+            copy.wait_send()
     for piece, (source, target) in enumerate(pieces):
         for y, z in peers:
             index = y * nz + z
@@ -382,8 +384,6 @@
             ).wait_recv()
     for copy in own_copies:
         copy.wait()
-    for copy in started:
-        copy.wait_send()
 
 
 def spread_weights(last_up, last_down, first_up, first_down):

time: 474 us -> 476 us (level)
  the two profiles are of different devices: /device:TPU:4 before, /device:TPU:38 now
where the time goes in v7:
time: 476 us; the launch traced here: 467 us
  Pallas kernels  382 us (80%)
  other arithmetic  29 us (6%)
  matrix products  18.3 us (4%)
  between operations  17.7 us (4%)
  starting transfers between devices  10.4 us (2%)
  local copies, waits for them, and re-layouts  9.15 us (2%)
    pallas_call x1, Pallas kernels, spread_weights(): pl.pallas_call(functools.partial(spread_kernel, ny, nz), out_shape=(up_sh...  186 us
    pallas_call x2, Pallas kernels, reduce_columns(): pl.pallas_call(functools.partial(scatter_kernel, ny, nz), out_shape=jax.S...  107 us
    pallas_call x4, Pallas kernels, row_sums(): pl.pallas_call(functools.partial(sum_kernel, ny, nz), out_shape=jax.Shape...  47.4 us
    pallas_call x2, Pallas kernels, gather_columns(): pl.pallas_call(functools.partial(gather_kernel, ny, nz), out_shape=jax.Sh...  41.7 us
    ppermute x2, starting transfers between devices, shifted(): lax.ppermute(value, axis, [(source, source + steps) for source in range(i...  10.4 us
  transfers between devices with their start and end apart: 2, of which 0 were waited for; matrix products, arithmetic and copies ran while one was open for 3% of the time, Pallas kernels for 2%

profile of v7, /device:TPU:38, one launch (start us, length us, event | category | flops | bytes accessed | tf_op | source)
XLA Modules:
  0.0 466.7 jit_solution(15475655439654435612)
XLA Ops:
  0.7 1.2 fusion.32
  1.9 1.7 fusion.33
  4.2 13.3 %shard_map.176 = f32[6,128]{1,0:T(8,128)} custom-call(f32[6,128]{1,0:T(8,128)} %reshape.220.v_ref), custom_call_target="tpu_custom_call" | custom-call | flops 6144 | bytes 49152 | tf_op jit(solution)/shard_map/pallas_call | solution.py:309
  17.6 0.7 reshape_reshape.3
  18.3 186.2 %shard_map.177 = (bf16[1024,1024]{1,0:T(8,128)(2,1)}, bf16[1024,1024]{1,0:T(8,128)(2,1)}, bf16[1024,1024]{1,0:T(8,128)(2,1)}, bf16[1024,1024]{1,0:T(8,128)(2,1)}) custom-call(bf16[8192,128]{1,0:T(8,128)(2,1)} %bitcast.177, bf16[128,8192]{1,0:T(8,128)(2,1)} %bitcast.178, bf16[8192,128]{1,0:T(8,128)(2,1)} %bitcast.179, bf16[128,8192]{1,0:T(8,128)(2,1)} %bitcast.180), custom_call_target="tpu_custom_call" | custom-call | bytes 8388608 | tf_op jit(solution)/shard_map/pallas_call | solution.py:396
  204.5 3.5 convolution_bitcast_fusion.3
  207.9 0.9 constant_dynamic-slice_fusion
  208.8 2.4 convolution_bitcast_fusion.4
  211.2 0.8 convolution_bitcast_fusion.5
  212.4 2.1 pad_maximum_fusion.part_ref
  214.5 46.8 %shard_map.178 = f32[3,256,128]{2,1,0:T(8,128)} custom-call(f32[3,256,1024]{2,1,0:T(8,128)} %pad_maximum_fusion.part_ref), custom_call_target="tpu_custom_call" | custom-call | flops 786432 | bytes 3145728 | tf_op jit(solution)/shard_map/pallas_call | solution.py:241
  261.3 1.1 multiply_convert_fusion.4
  262.5 21.0 %shard_map.179 = bf16[2,256,1024]{2,1,0:T(8,128)(2,1)S(1)} custom-call(bf16[2,256,128]{2,1,0:T(8,128)(2,1)S(1)} %pad_maximum_fusion.2.x_ref), custom_call_target="tpu_custom_call" | custom-call | bytes 917504 | tf_op jit(solution)/shard_map/pallas_call | solution.py:135
  283.6 1.3 convert_reduce_fusion.2
  286.9 1.2 convert_reduce_fusion.3
  288.1 0.8 fusion.86
  289.3 2.0 dynamic-slice_multiply_fusion
  291.5 0.8 maximum_bitcast_fusion
  292.8 11.3 %shard_map.180 = f32[3,128]{1,0:T(4,128)} custom-call(f32[3,128]{1,0:T(4,128)} %fusion.65.v_ref), custom_call_target="tpu_custom_call" | custom-call | flops 3072 | bytes 24576 | tf_op jit(solution)/shard_map/pallas_call | solution.py:309
  304.2 0.8 slice_bitcast_fusion.4
  305.0 2.6 fusion.26
  307.5 8.3 %collective-permute-start.1 = (bf16[256,1024]{1,0:T(8,128)(2,1)}, bf16[256,1024]{1,0:T(8,128)(2,1)}, u32[]{:S(2)}, u32[]{:S(2)}) collective-permute-start(bf16[256,1024]{1,0:T(8,128)(2,1)} %fusion.26), channel_id=1, source_target_pairs={{8,0},{16,8},{24,16},{32,24},{40,32},{48,40},{56,48},{64,56},{72,6... | collective-permute-start | bytes 1572872 | tf_op jit(solution)/shard_map/ppermute | solution.py:20
  316.0 2.1 collective-permute-start
  318.1 0.7 slice_bitcast_fusion.5
  320.1 0.7 fusion.89
  320.8 0.7 fusion.88
  336.5 2.0 multiply_reduce_fusion
  338.5 1.7 convolution_bitcast_fusion.1
  340.2 1.3 fusion.34
  341.6 1.2 fusion.64.v_ref
  342.7 0.7 broadcast_divide_fusion.1
  343.4 11.5 %shard_map.181 = f32[3,128]{1,0:T(4,128)} custom-call(f32[3,128]{1,0:T(4,128)} %fusion.64.v_ref), custom_call_target="tpu_custom_call" | custom-call | flops 3072 | bytes 24576 | tf_op jit(solution)/shard_map/pallas_call | solution.py:309
  354.9 0.8 rsqrt_bitcast_fusion
  355.7 1.2 slice.117
  356.9 2.0 subtract_multiply_fusion
  358.9 2.4 convolution_bitcast_fusion.2
  361.3 1.9 convolution_bitcast_fusion
  363.3 1.9 pad_maximum_fusion.1.part_ref
  365.2 60.0 %shard_map.182 = f32[3,256,128]{2,1,0:T(8,128)} custom-call(f32[3,256,1024]{2,1,0:T(8,128)} %pad_maximum_fusion.1.part_ref), custom_call_target="tpu_custom_call" | custom-call | flops 786432 | bytes 3145728 | tf_op jit(solution)/shard_map/pallas_call | solution.py:241
  425.2 1.1 multiply_convert_fusion.2
  426.4 20.8 %shard_map.183 = bf16[2,256,1024]{2,1,0:T(8,128)(2,1)S(1)} custom-call(bf16[2,256,128]{2,1,0:T(8,128)(2,1)S(1)} %pad_maximum_fusion.3.x_ref), custom_call_target="tpu_custom_call" | custom-call | bytes 917504 | tf_op jit(solution)/shard_map/pallas_call | solution.py:135
  447.3 1.2 convert_reduce_fusion.1
  448.5 1.0 fusion.39
  449.6 1.3 convert_reduce_fusion
  450.9 1.0 copy-done.9
  451.9 0.9 fusion.16
  452.7 11.3 %shard_map.184 = f32[2,128]{1,0:T(2,128)} custom-call(f32[2,128]{1,0:T(2,128)} %bitcast.211), custom_call_target="tpu_custom_call" | custom-call | flops 2048 | bytes 16384 | tf_op jit(solution)/shard_map/pallas_call | solution.py:309
  464.1 2.6 fusion.45
  (59 shorter events, 4.5 us)
Async XLA Ops:
  0.6 290.7 %copy-start = (f32[1024,4]{0,1:T(4,128)S(1)}, f32[1024,4]{0,1:T(4,128)}, u32[]{:S(2)}) copy-start(f32[1024,4]{0,1:T(4,128)} %param.29) | copy-start | bytes 49156
  18.3 186.2 %copy-start.12 = (bf16[1,256,1024]{2,1,0:T(8,128)(2,1)S(1)}, bf16[1,256,1024]{2,1,0:T(8,128)(2,1)}, u32[]{:S(2)}) copy-start(bf16[1,256,1024]{2,1,0:T(8,128)(2,1)} %param.20) | copy-start | bytes 1572868
  204.5 4.3 copy-start.3
  207.9 3.2 copy-start.1
  207.9 3.2 copy-start.4
  211.2 1.2 copy-start.11
  262.4 21.2 %copy-start.2 = (bf16[1024,1024]{1,0:T(8,128)(2,1)S(1)}, bf16[1024,1024]{1,0:T(8,128)(2,1)}, u32[]{:S(2)}) copy-start(bf16[1024,1024]{1,0:T(8,128)(2,1)} %get-tuple-element.17) | copy-start | bytes 6291460
  284.9 3.2 copy-start.6
  284.9 2.0 copy-start.16
  286.4 1.7 copy-start.13
  288.1 1.2 copy-start.7
  304.1 11.7 %copy-start.5 = (bf16[1,256,1024]{2,1,0:T(8,128)(2,1)S(1)}, bf16[1,256,1024]{2,1,0:T(8,128)(2,1)}, u32[]{:S(2)}) copy-start(bf16[1,256,1024]{2,1,0:T(8,128)(2,1)} %param.17) | copy-start | bytes 1572868
  304.2 11.7 %copy-start.8 = (f32[256,1024]{1,0:T(8,128)S(1)}, f32[256,1024]{1,0:T(8,128)}, u32[]{:S(2)}) copy-start(f32[256,1024]{1,0:T(8,128)} %copy-done.7) | copy-start | bytes 3145732
  304.9 15.1 %copy-start.14 = (f32[4]{0:T(128)S(1)}, f32[4]{0:T(128)}, u32[]{:S(2)}) copy-start(f32[4]{0:T(128)} %param.30) | copy-start | bytes 52
  305.0 15.8 %copy-start.18 = (s32[1,4]{1,0:T(1,128)S(1)}, s32[1,4]{1,0:T(1,128)}, u32[]{:S(2)}) copy-start(s32[1,4]{1,0:T(1,128)} %param.33) | copy-start | bytes 52
  307.5 53.8 %collective-permute-start.1 = (bf16[256,1024]{1,0:T(8,128)(2,1)}, bf16[256,1024]{1,0:T(8,128)(2,1)}, u32[]{:S(2)}, u32[]{:S(2)}) collective-permute-start(bf16[256,1024]{1,0:T(8,128)(2,1)} %fusion.26), channel_id=1, source_target_pairs={{8,0},{16,8},{24,16},{32,24},{40,32},{48,40},{56,48},{64,56},{72,6... | collective-permute-start | bytes 1572872 | tf_op jit(solution)/shard_map/ppermute | solution.py:20
  316.0 24.2 %collective-permute-start = (bf16[256,1024]{1,0:T(8,128)(2,1)S(1)}, bf16[256,1024]{1,0:T(8,128)(2,1)}, u32[]{:S(2)}, u32[]{:S(2)}) collective-permute-start(bf16[256,1024]{1,0:T(8,128)(2,1)S(1)} %fusion.30), channel_id=1, source_target_pairs={{0,8},{8,16},{16,24},{24,32},{32,40},{40,48},{48,56},{56,64},{64,7... | collective-permute-start | bytes 1572872 | tf_op jit(solution)/shard_map/ppermute | solution.py:20
  354.9 6.4 %copy-start.17 = (bf16[1024,1024]{1,0:T(8,128)(2,1)S(1)}, bf16[1024,1024]{1,0:T(8,128)(2,1)}, u32[]{:S(2)}) copy-start(bf16[1024,1024]{1,0:T(8,128)(2,1)} %get-tuple-element.19) | copy-start | bytes 6291460
  361.3 2.0 copy-start.10
  426.3 21.0 %copy-start.15 = (bf16[1024,1024]{1,0:T(8,128)(2,1)S(1)}, bf16[1024,1024]{1,0:T(8,128)(2,1)}, u32[]{:S(2)}) copy-start(bf16[1024,1024]{1,0:T(8,128)(2,1)} %get-tuple-element.18) | copy-start | bytes 6291460
  450.9 1.0 copy-start.9

commit v8 on v5

--- a/solution.py
+++ b/solution.py
@@ -168,7 +168,7 @@
     pl.semaphore_wait(barrier, ny)
 
     sends = []
-    for step in range(1, ny):
+    for step in sorted(range(1, ny), key=lambda s: -min(s, ny - s)):
         peer = lax.rem(ty + step, ny)
         copy = pltpu.make_async_remote_copy(
             src_ref=part_ref.at[:, :, pl.ds(pl.multiple_of(peer * pair, pair), pair)],

time: 462 us -> 462 us (level)
  no operation moved by 1% of the time
where the time goes in v8:
time: 462 us; the launch traced here: 460 us
  Pallas kernels  204 us (44%)
  waiting for transfers between devices  75 us (16%)
  blocking collectives  60.4 us (13%)
  local copies, waits for them, and re-layouts  35.9 us (8%)
  other arithmetic  27.8 us (6%)
  starting transfers between devices  20.7 us (4%)
  matrix products  18.3 us (4%)
  between operations  17.3 us (4%)
    pallas_call x2, Pallas kernels, reduce_columns(): pl.pallas_call(functools.partial(scatter_kernel, ny, nz), out_shape=jax.S...  124 us
    all_to_all x1, blocking collectives, spread_weights(): lax.all_to_all(up_matrix.reshape(n, width, hidden), TENSOR, 0, 0, tiled=T...  60.4 us
    pallas_call x4, Pallas kernels, row_sums(): pl.pallas_call(functools.partial(sum_kernel, ny, nz), out_shape=jax.Shape...  48 us
    all_to_all x1, waiting for transfers between devices, spread_weights(): lax.all_to_all(up_matrix.reshape(n, width, hidden), TENSOR, 0, 0, tiled=T...  37.6 us
    all_to_all x2, waiting for transfers between devices, spread_weights(): lax.all_to_all(down_blocks, TENSOR, 0, 0, tiled=True)  37.4 us
    pallas_call x2, Pallas kernels, gather_columns(): pl.pallas_call(functools.partial(gather_kernel, ny, nz), out_shape=jax.Sh...  32.2 us
    unnamed x48, local copies, waits for them, and re-layouts  14.7 us
    all_to_all x2, starting transfers between devices, spread_weights(): lax.all_to_all(down_blocks, TENSOR, 0, 0, tiled=True)  11.2 us
  transfers between devices with their start and end apart: 5, of which 2 were waited for; matrix products, arithmetic and copies ran while one was open for 9% of the time, Pallas kernels for 21%

profile of v8, /device:TPU:38, one launch (start us, length us, event | category | flops | bytes accessed | tf_op | source)
XLA Modules:
  0.0 459.7 jit_solution(9949517340375314927)
XLA Ops:
  0.7 1.4 fusion.24
  2.0 1.7 fusion.27
  4.4 13.3 %shard_map.176 = f32[6,128]{1,0:T(8,128)} custom-call(f32[6,128]{1,0:T(8,128)} %reshape.274.v_ref), custom_call_target="tpu_custom_call" | custom-call | flops 6144 | bytes 49152 | tf_op jit(solution)/shard_map/pallas_call | solution.py:309
  18.4 2.4 copy.24
  20.8 4.2 copy.25
  25.1 60.4 %all_to_all.20 = bf16[8,1024,128]{2,1,0:T(8,128)(2,1)} all-to-all(bf16[8,1024,128]{2,1,0:T(8,128)(2,1)S(1)} %bitcast.224), channel_id=1, replica_groups=mesh['section'=32,'ty'=4,'tz'=2] {'ty','tz'}, dimensions={0} | all-to-all | bytes 4194304 | tf_op jit(solution)/shard_map/all_to_all | solution.py:329
  85.5 3.6 all-to-all-start.1
  89.1 4.0 copy.28
  93.1 37.6 %all-to-all-done.1 = bf16[8,1024,128]{2,1,0:T(8,128)(2,1)S(1)} async-done(((bf16[8,1024,128]{2,1,0:T(8,128)(2,1)}), bf16[8,1024,128]{2,1,0:T(8,128)(2,1)S(1)}, u32[]{:S(2)}, u32[]{:S(2)}) %all-to-all-start.1) | async-done | bytes 2097184 | tf_op jit(solution)/shard_map/all_to_all | solution.py:329
  130.7 1.3 copy-done.4
  132.0 6.7 %all-to-all-start.2 = ((bf16[8,128,1024]{2,1,0:T(8,128)(2,1)}), bf16[8,128,1024]{2,1,0:T(8,128)(2,1)}, u32[]{:S(2)}, u32[]{:S(2)}) async-start(bf16[8,128,1024]{2,1,0:T(8,128)(2,1)} %bitcast.222), calls=%async_computation.2 | async-start | bytes 4194304 | tf_op jit(solution)/shard_map/all_to_all | solution.py:332
  138.7 3.9 copy.30
  142.7 37.4 %all-to-all-done.2 = bf16[8,128,1024]{2,1,0:T(8,128)(2,1)} async-done(((bf16[8,128,1024]{2,1,0:T(8,128)(2,1)}), bf16[8,128,1024]{2,1,0:T(8,128)(2,1)}, u32[]{:S(2)}, u32[]{:S(2)}) %all-to-all-start.2) | async-done | bytes 2097184 | tf_op jit(solution)/shard_map/all_to_all | solution.py:332
  180.1 4.5 all-to-all-start.3
  190.6 2.9 copy.27
  193.5 4.0 copy.26
  197.5 2.4 convolution_bitcast_fusion.3
  202.3 2.1 pad_maximum_fusion.part_ref
  204.4 67.7 %shard_map.177 = f32[3,256,128]{2,1,0:T(8,128)} custom-call(f32[3,256,1024]{2,1,0:T(8,128)} %pad_maximum_fusion.part_ref), custom_call_target="tpu_custom_call" | custom-call | flops 786432 | bytes 3145728 | tf_op jit(solution)/shard_map/pallas_call | solution.py:241
  272.1 1.1 multiply_convert_fusion.4
  273.3 15.9 %shard_map.178 = bf16[2,256,1024]{2,1,0:T(8,128)(2,1)S(1)} custom-call(bf16[2,256,128]{2,1,0:T(8,128)(2,1)S(1)} %pad_maximum_fusion.2.x_ref), custom_call_target="tpu_custom_call" | custom-call | bytes 917504 | tf_op jit(solution)/shard_map/pallas_call | solution.py:135
  289.2 0.9 copy.36
  290.9 1.2 convert_reduce_fusion.2
  292.2 1.0 copy-done.10
  293.5 3.1 convert_reduce_fusion.3
  296.9 2.0 dynamic-slice_multiply_fusion
  300.4 1.0 fusion.31
  301.4 11.4 %shard_map.179 = f32[3,128]{1,0:T(4,128)} custom-call(f32[3,128]{1,0:T(4,128)} %fusion.67.v_ref), custom_call_target="tpu_custom_call" | custom-call | flops 3072 | bytes 24576 | tf_op jit(solution)/shard_map/pallas_call | solution.py:309
  328.3 2.1 collective-permute-start
  330.4 2.7 fusion.23
  333.1 3.8 collective-permute-start.1
  337.2 2.0 multiply_reduce_fusion
  339.5 1.2 fusion.66.v_ref
  340.7 1.8 convolution_bitcast_fusion.1
  342.4 12.0 %shard_map.180 = f32[3,128]{1,0:T(4,128)} custom-call(f32[3,128]{1,0:T(4,128)} %fusion.66.v_ref), custom_call_target="tpu_custom_call" | custom-call | flops 3072 | bytes 24576 | tf_op jit(solution)/shard_map/pallas_call | solution.py:309
  355.1 1.2 slice.117
  356.2 2.0 subtract_multiply_fusion
  359.1 2.6 convolution_bitcast_fusion
  361.7 2.0 pad_maximum_fusion.1.part_ref
  363.7 56.4 %shard_map.181 = f32[3,256,128]{2,1,0:T(8,128)} custom-call(f32[3,256,1024]{2,1,0:T(8,128)} %pad_maximum_fusion.1.part_ref), custom_call_target="tpu_custom_call" | custom-call | flops 786432 | bytes 3145728 | tf_op jit(solution)/shard_map/pallas_call | solution.py:241
  420.1 1.1 multiply_convert_fusion.2
  421.3 16.3 %shard_map.182 = bf16[2,256,1024]{2,1,0:T(8,128)(2,1)S(1)} custom-call(bf16[2,256,128]{2,1,0:T(8,128)(2,1)S(1)} %pad_maximum_fusion.3.x_ref), custom_call_target="tpu_custom_call" | custom-call | bytes 917504 | tf_op jit(solution)/shard_map/pallas_call | solution.py:135
  438.6 1.2 convert_reduce_fusion
  439.9 1.0 copy-done.8
  441.7 11.3 %shard_map.183 = f32[2,128]{1,0:T(2,128)} custom-call(f32[2,128]{1,0:T(2,128)} %bitcast.255), custom_call_target="tpu_custom_call" | custom-call | flops 2048 | bytes 16384 | tf_op jit(solution)/shard_map/pallas_call | solution.py:309
  453.0 1.1 copy.38
  454.2 3.0 convert_reduce_fusion.1
  457.2 2.5 fusion.45
  (73 shorter events, 15.9 us)
Async XLA Ops:
  0.6 187.9 %copy-start = (f32[1,8192]{1,0:T(1,128)S(1)}, f32[1,8192]{1,0:T(1,128)}, u32[]{:S(2)}) copy-start(f32[1,8192]{1,0:T(1,128)} %param.22) | copy-start | bytes 98308
  0.6 17.7 %copy-start.12 = (bf16[1,128,8192]{2,1,0:T(8,128)(2,1)S(1)}, bf16[1,128,8192]{2,1,0:T(8,128)(2,1)}, u32[]{:S(2)}) copy-start(bf16[1,128,8192]{2,1,0:T(8,128)(2,1)} %param.24) | copy-start | bytes 6291460
  20.8 4.2 copy-start.13
  85.5 45.2 %all-to-all-start.1 = ((bf16[8,1024,128]{2,1,0:T(8,128)(2,1)}), bf16[8,1024,128]{2,1,0:T(8,128)(2,1)S(1)}, u32[]{:S(2)}, u32[]{:S(2)}) async-start(bf16[8,1024,128]{2,1,0:T(8,128)(2,1)} %bitcast.225), calls=%async_computation.1 | async-start | bytes 4194304 | tf_op jit(solution)/shard_map/all_to_all | solution.py:329
  130.7 1.3 copy-start.4
  132.0 48.1 %all-to-all-start.2 = ((bf16[8,128,1024]{2,1,0:T(8,128)(2,1)}), bf16[8,128,1024]{2,1,0:T(8,128)(2,1)}, u32[]{:S(2)}, u32[]{:S(2)}) async-start(bf16[8,128,1024]{2,1,0:T(8,128)(2,1)} %bitcast.222), calls=%async_computation.2 | async-start | bytes 4194304 | tf_op jit(solution)/shard_map/all_to_all | solution.py:332
  180.1 5.1 %copy-start.19 = (s32[1,4]{1,0:T(1,128)S(1)}, s32[1,4]{1,0:T(1,128)}, u32[]{:S(2)}) copy-start(s32[1,4]{1,0:T(1,128)} %param.33) | copy-start | bytes 52
  180.1 9.1 %copy-start.17 = (s32[1,256]{1,0:T(1,128)S(1)}, s32[1,256]{1,0:T(1,128)}, u32[]{:S(2)}) copy-start(s32[1,256]{1,0:T(1,128)} %param.32) | copy-start | bytes 3076
  180.1 113.4 %all-to-all-start.3 = ((bf16[8,128,1024]{2,1,0:T(8,128)(2,1)}), bf16[8,128,1024]{2,1,0:T(8,128)(2,1)}, u32[]{:S(2)}, u32[]{:S(2)}) async-start(bf16[8,128,1024]{2,1,0:T(8,128)(2,1)} %bitcast.31), calls=%async_computation.3 | async-start | bytes 4194304 | tf_op jit(solution)/shard_map/all_to_all | solution.py:332
  193.5 4.0 copy-start.14
  197.5 2.4 copy-start.7
  199.9 1.6 copy-start.1
  199.9 1.7 copy-start.6
  289.2 1.8 copy-start.5
  292.2 1.0 copy-start.10
  293.5 5.4 %copy-start.15 = (f32[1024,4]{0,1:T(4,128)S(1)}, f32[1024,4]{0,1:T(4,128)}, u32[]{:S(2)}) copy-start(f32[1024,4]{0,1:T(4,128)} %param.29) | copy-start | bytes 49156
  296.6 18.8 %copy-start.18 = (f32[4]{0:T(128)S(1)}, f32[4]{0:T(128)}, u32[]{:S(2)}) copy-start(f32[4]{0:T(128)} %param.30) | copy-start | bytes 52
  328.3 12.4 %copy-start.2 = (bf16[1024,8,128]{0,2,1:T(8,128)(2,1)S(1)}, bf16[1024,8,128]{0,2,1:T(8,128)(2,1)}, u32[]{:S(2)}) copy-start(bf16[1024,8,128]{0,2,1:T(8,128)(2,1)} %copy.26) | copy-start | bytes 6291460
  328.3 10.9 %collective-permute-start = (bf16[256,1024]{1,0:T(8,128)(2,1)}, bf16[256,1024]{1,0:T(8,128)(2,1)S(1)}, u32[]{:S(2)}, u32[]{:S(2)}) collective-permute-start(bf16[256,1024]{1,0:T(8,128)(2,1)} %fusion.31), channel_id=1, source_target_pairs={{0,8},{8,16},{16,24},{24,32},{32,40},{40,48},{48,56},{56,64},{64,7... | collective-permute-start | bytes 1572872 | tf_op jit(solution)/shard_map/ppermute | solution.py:20
  333.1 26.0 %collective-permute-start.1 = (bf16[256,1024]{1,0:T(8,128)(2,1)}, bf16[256,1024]{1,0:T(8,128)(2,1)}, u32[]{:S(2)}, u32[]{:S(2)}) collective-permute-start(bf16[256,1024]{1,0:T(8,128)(2,1)} %fusion.23), channel_id=1, source_target_pairs={{8,0},{16,8},{24,16},{32,24},{40,32},{48,40},{56,48},{64,56},{72,6... | collective-permute-start | bytes 1572872 | tf_op jit(solution)/shard_map/ppermute | solution.py:20
  359.0 2.6 copy-start.11
  421.3 17.3 %copy-start.3 = (bf16[8,1024,128]{2,1,0:T(8,128)(2,1)S(1)}, bf16[8,1024,128]{2,1,0:T(8,128)(2,1)}, u32[]{:S(2)}) copy-start(bf16[8,1024,128]{2,1,0:T(8,128)(2,1)} %all_to_all.20) | copy-start | bytes 6291460
  439.9 1.0 copy-start.8
  454.2 3.0 copy-start.9
  454.2 3.0 copy-start.16
